TPU v7x, 512 devices: a whole 4x4x16 slice. The times are simulated.
512 devices in a mesh: slab: 16 (over y, x), row: 32 (over z, core).
Axes of the slice: x: 4, y: 4, z: 16, core: 2. Of those that a mesh axis runs over, the one named last changes fastest.
Arguments:
- atom_feats: bfloat16 [128, 524288], P(None, ('slab', 'row')), may hold values from -6 to 6
- cotangent: bfloat16 [128, 524288], P(None, ('slab', 'row')), may hold values from -6 to 6
- filter_modes: bfloat16 [128, 256, 2, 256], P('row', 'slab'), may hold values from -5 to 5
- block_tiles: int32 [16384, 1], P(('slab', 'row')), may hold values from 0 to 31, as said below
- cell_offsets: int32 [524288], P(('slab', 'row')), may hold values from 0 to 511
- live_counts: int32 [512], P(('slab', 'row')), may hold values from 256 to 1024, as said below
Outputs:
- long_range: bfloat16 [128, 524288], P(None, ('slab', 'row'))
- grad_feats: bfloat16 [128, 524288], P(None, ('slab', 'row'))
- grad_filter: float32 [128, 256, 2, 256], P('row', 'slab')
Inputs may be any that keep to these rules, and one draw needn't show every extreme that they name: `block_tiles`: in each brick's 32 blocks (the rows of one device) no x-row index appears more than 2 times; in every slab one x-row index appears exactly 2 times in every brick of that slab. `live_counts`: some brick has all 1024 slots live.
All inputs are finite; a program needn't handle non-finite values.
Results may differ from a plain program's by a relative error of at most 0.014.
Values may be sent and summed in bfloat16 or wider, within the bound.
No kernel may reach another device: no remote copies, remote signals or barrier semaphores. Data moves between devices by JAX's collectives and lax.ppermute only.
A program may use at most 64 MiB of HBM per device.

v0:
```python
import jax
import jax.numpy as jnp
from jax import lax
from jax.sharding import PartitionSpec as P

C = 128
NX = 256
NZ = 256
NY = 4
BLK = 32


def trig_table(length):
    positions = jnp.arange(length, dtype=jnp.int32)
    angles = (positions[:, None] * positions[None, :] % length).astype(jnp.float32) * (
        2.0 * jnp.pi / length
    )
    return (jnp.cos(angles), jnp.sin(angles))


def make_tables():
    cos_x, sin_x = trig_table(NX)
    cos_z, sin_z = trig_table(NZ)
    inverse_size = 1.0 / (NX * NZ)
    table_fwd = jnp.concatenate([cos_x, -sin_x], axis=1).astype(jnp.bfloat16)
    table_inv = (jnp.concatenate([cos_x, -sin_x], axis=0) * inverse_size).astype(jnp.bfloat16)
    upper_half = jnp.concatenate([cos_z, -sin_z], axis=1)
    lower_half = jnp.concatenate([sin_z, cos_z], axis=1)
    table_z = jnp.concatenate([upper_half, lower_half], axis=0).astype(jnp.bfloat16)
    return (table_fwd, table_inv, table_z)


def spread(cell_index, values, total_cells):
    summed = (
        jnp.zeros((values.shape[0], total_cells), jnp.float32)
        .at[:, cell_index]
        .add(values.astype(jnp.float32))
    )
    return summed.astype(jnp.bfloat16)


def rows_from_tiles(tiles, row_count, slab_rows, row_cols):
    chan_local = tiles.shape[0] // row_count
    arranged = tiles.reshape(row_count, chan_local, slab_rows, NY, row_cols).transpose(
        1, 2, 3, 0, 4
    )
    return arranged.reshape(chan_local * slab_rows * NY, row_count * row_cols)


def tiles_from_rows(rows_in, row_count, slab_rows, row_cols):
    chan_local = rows_in.shape[0] // (slab_rows * NY)
    arranged = rows_in.reshape(chan_local, slab_rows, NY, row_count, row_cols).transpose(
        3, 0, 1, 2, 4
    )
    return arranged.reshape(row_count * chan_local, slab_rows * NY * row_cols)


def to_columns(rows_in, slab_count, slab_rows):
    chan_local = rows_in.shape[0] // (slab_rows * NY)
    kx_local = NX // slab_count
    arranged = rows_in.reshape(chan_local, slab_rows, NY, 2, slab_count, kx_local).transpose(
        4, 0, 2, 5, 3, 1
    )
    return arranged.reshape(slab_count, chan_local * NY * kx_local * 2 * slab_rows)


def from_columns(received, slab_count, slab_rows, chan_local):
    kx_local = NX // slab_count
    arranged = received.reshape(slab_count, chan_local, NY, kx_local, 2, slab_rows).transpose(
        1, 2, 3, 4, 0, 5
    )
    return arranged.reshape(chan_local * NY * kx_local, 2 * NZ)


def to_planes(columns, slab_count, slab_rows, chan_local):
    kx_local = NX // slab_count
    arranged = columns.reshape(chan_local, NY, kx_local, 2, slab_count, slab_rows).transpose(
        4, 0, 1, 2, 3, 5
    )
    return arranged.reshape(slab_count, chan_local * NY * kx_local * 2 * slab_rows)


def from_planes(received, slab_count, slab_rows, chan_local):
    kx_local = NX // slab_count
    arranged = received.reshape(slab_count, chan_local, NY, kx_local, 2, slab_rows).transpose(
        1, 5, 2, 4, 0, 3
    )
    return arranged.reshape(chan_local * slab_rows * NY, 2 * NX)


def on_device(atom_feats, cotangent, filter_modes, block_tiles, cell_offsets, live_counts):
    row_count = lax.axis_size("row")
    slab_count = lax.axis_size("slab")
    slab_rows = NZ // slab_count
    row_cols = NX // row_count
    chan_local = C // row_count
    kx_local = NX // slab_count
    atoms_dev = atom_feats.shape[1]
    blocks_dev = atoms_dev // BLK
    tile_cells = slab_rows * NY * row_cols
    live_mask = jnp.arange(atoms_dev, dtype=jnp.int32) < live_counts[0]
    feats_live = jnp.where(live_mask[None, :], atom_feats, jnp.zeros_like(atom_feats))
    cot_live = jnp.where(live_mask[None, :], cotangent, jnp.zeros_like(cotangent))
    targets = block_tiles[:, 0]
    table_fwd, table_inv, table_z = make_tables()
    capacity = max(2, 2 * blocks_dev // row_count)
    slot_count = row_count * capacity
    target_hits = (targets[:, None] == jnp.arange(row_count, dtype=jnp.int32)[None, :]).astype(
        jnp.int32
    )
    before = jnp.sum((jnp.cumsum(target_hits, axis=0) - target_hits) * target_hits, axis=1)
    slot_of = targets * capacity + before
    owner_block = (
        jnp.full((slot_count,), -1, jnp.int32)
        .at[slot_of]
        .set(jnp.arange(blocks_dev, dtype=jnp.int32))
    )
    filled = owner_block >= 0
    source = jnp.maximum(owner_block, 0)

    def pack_slots(values):
        blocks = values.reshape(values.shape[0], blocks_dev, BLK)
        chosen = jnp.take(blocks, source, axis=1)
        chosen = jnp.where(filled[None, :, None], chosen, jnp.zeros_like(chosen))
        return chosen.reshape(values.shape[0], slot_count * BLK)

    send_offsets = jnp.take(cell_offsets.reshape(blocks_dev, BLK), source, axis=0).reshape(
        slot_count * BLK
    )
    got_feats, got_cot = (
        lax.all_to_all(pack_slots(feats_live), "row", split_axis=1, concat_axis=1, tiled=True),
        lax.all_to_all(pack_slots(cot_live), "row", split_axis=1, concat_axis=1, tiled=True),
    )
    got_cells = lax.all_to_all(send_offsets, "row", split_axis=0, concat_axis=0, tiled=True)
    tile_feats = spread(got_cells, got_feats, tile_cells)
    tile_cot = spread(got_cells, got_cot, tile_cells)
    tile_feats, tile_cot = (
        lax.all_to_all(tile_feats, "row", split_axis=0, concat_axis=0, tiled=True),
        lax.all_to_all(tile_cot, "row", split_axis=0, concat_axis=0, tiled=True),
    )
    mesh_feats = rows_from_tiles(tile_feats, row_count, slab_rows, row_cols)
    mesh_cot = rows_from_tiles(tile_cot, row_count, slab_rows, row_cols)
    row_feats = jnp.dot(mesh_feats, table_fwd, preferred_element_type=jnp.float32).astype(
        jnp.bfloat16
    )
    row_cot = jnp.dot(mesh_cot, table_inv.T, preferred_element_type=jnp.float32).astype(
        jnp.bfloat16
    )
    col_feats, col_cot = (
        lax.all_to_all(
            to_columns(row_feats, slab_count, slab_rows),
            "slab",
            split_axis=0,
            concat_axis=0,
            tiled=True,
        ),
        lax.all_to_all(
            to_columns(row_cot, slab_count, slab_rows),
            "slab",
            split_axis=0,
            concat_axis=0,
            tiled=True,
        ),
    )
    spectrum = jnp.dot(
        from_columns(col_feats, slab_count, slab_rows, chan_local),
        table_z,
        preferred_element_type=jnp.float32,
    ).astype(jnp.bfloat16)
    cot_filtered = jnp.dot(
        from_columns(col_cot, slab_count, slab_rows, chan_local),
        table_z,
        preferred_element_type=jnp.float32,
    ).astype(jnp.bfloat16)
    spec_five = spectrum.reshape(chan_local, NY, kx_local, 2, NZ).astype(jnp.float32)
    grad_five = cot_filtered.reshape(chan_local, NY, kx_local, 2, NZ).astype(jnp.float32)
    real_s = spec_five[:, :, :, 0, :]
    imag_s = spec_five[:, :, :, 1, :]
    real_g = grad_five[:, :, :, 0, :]
    imag_g = grad_five[:, :, :, 1, :]
    filter_f32 = filter_modes.astype(jnp.float32)
    real_f = filter_f32[:, None, :, 0, :]
    imag_f = filter_f32[:, None, :, 1, :]
    filtered = jnp.stack(
        [real_s * real_f - imag_s * imag_f, real_s * imag_f + imag_s * real_f], axis=3
    )
    filtered = filtered.astype(jnp.bfloat16).reshape(chan_local * NY * kx_local, 2 * NZ)
    grad_filter = jnp.stack(
        [
            jnp.sum(real_g * real_s + imag_g * imag_s, axis=1),
            jnp.sum(imag_g * real_s - real_g * imag_s, axis=1),
        ],
        axis=2,
    )
    cot_spectrum = jnp.stack(
        [real_g * real_f + imag_g * imag_f, imag_g * real_f - real_g * imag_f], axis=3
    )
    cot_spectrum = cot_spectrum.astype(jnp.bfloat16).reshape(chan_local * NY * kx_local, 2 * NZ)
    planes = jnp.dot(filtered, table_z.T, preferred_element_type=jnp.float32).astype(jnp.bfloat16)
    cot_planes = jnp.dot(cot_spectrum, table_z.T, preferred_element_type=jnp.float32).astype(
        jnp.bfloat16
    )
    back_feats, back_cot = (
        lax.all_to_all(
            to_planes(planes, slab_count, slab_rows, chan_local),
            "slab",
            split_axis=0,
            concat_axis=0,
            tiled=True,
        ),
        lax.all_to_all(
            to_planes(cot_planes, slab_count, slab_rows, chan_local),
            "slab",
            split_axis=0,
            concat_axis=0,
            tiled=True,
        ),
    )
    field_rows = jnp.dot(
        from_planes(back_feats, slab_count, slab_rows, chan_local),
        table_inv,
        preferred_element_type=jnp.float32,
    ).astype(jnp.bfloat16)
    cot_field = jnp.dot(
        from_planes(back_cot, slab_count, slab_rows, chan_local),
        table_fwd.T,
        preferred_element_type=jnp.float32,
    ).astype(jnp.bfloat16)
    field_tile, cot_tile = (
        lax.all_to_all(
            tiles_from_rows(field_rows, row_count, slab_rows, row_cols),
            "row",
            split_axis=0,
            concat_axis=0,
            tiled=True,
        ),
        lax.all_to_all(
            tiles_from_rows(cot_field, row_count, slab_rows, row_cols),
            "row",
            split_axis=0,
            concat_axis=0,
            tiled=True,
        ),
    )
    field_vals = jnp.take(field_tile, got_cells, axis=1)
    cot_vals = jnp.take(cot_tile, got_cells, axis=1)
    home_field, home_cot = (
        lax.all_to_all(field_vals, "row", split_axis=1, concat_axis=1, tiled=True),
        lax.all_to_all(cot_vals, "row", split_axis=1, concat_axis=1, tiled=True),
    )
    at_atoms = jnp.take(home_field.reshape(C, slot_count, BLK), slot_of, axis=1).reshape(
        C, atoms_dev
    )
    cot_atoms = jnp.take(home_cot.reshape(C, slot_count, BLK), slot_of, axis=1).reshape(
        C, atoms_dev
    )
    long_range = jnp.where(live_mask[None, :], at_atoms, jnp.zeros_like(at_atoms))
    grad_feats = jnp.where(live_mask[None, :], cot_atoms, jnp.zeros_like(cot_atoms))
    return (long_range, grad_feats, grad_filter)


def solution(mesh):
    in_specs = (
        P(None, ("slab", "row")),
        P(None, ("slab", "row")),
        P("row", "slab", None, None),
        P(("slab", "row"), None),
        P(("slab", "row")),
        P(("slab", "row")),
    )
    out_specs = (P(None, ("slab", "row")), P(None, ("slab", "row")), P("row", "slab", None, None))
    return jax.shard_map(
        on_device, mesh=mesh, in_specs=in_specs, out_specs=out_specs, check_vma=False
    )
```

profile of v0, /device:TPU:1, one launch (start us, length us, event | category | flops | bytes accessed | tf_op | source)
XLA Modules:
  0.0 438.4 jit_solution(8853404509354937251)
XLA Ops:
  6.6 16.7 %all-to-all-start = ((s32[32,64,1]{1,2,0:T(1,128)}), s32[32,64,1]{1,2,0:T(1,128)S(1)}, u32[]{:S(2)}, u32[]{:S(2)}) async-start(s32[32,64,1]{1,2,0:T(1,128)} %copy.69), calls=%async_computation | async-start | bytes 32768 | tf_op jit(solution)/shard_map/all_to_all | solution.py:134
  28.9 6.3 %all-to-all-done = s32[32,64,1]{1,2,0:T(1,128)S(1)} async-done(((s32[32,64,1]{1,2,0:T(1,128)}), s32[32,64,1]{1,2,0:T(1,128)S(1)}, u32[]{:S(2)}, u32[]{:S(2)}) %all-to-all-start) | async-done | bytes 8224 | tf_op jit(solution)/shard_map/all_to_all | solution.py:134
  35.1 39.4 %all_to_all.130 = bf16[128,32,64]{0,2,1:T(8,128)(2,1)S(1)} all-to-all(bf16[128,32,64]{0,2,1:T(8,128)(2,1)S(1)} %bitcast.128), channel_id=1, replica_groups=mesh['slab'=16,'row'=32] {'row'}, dimensions={1} | all-to-all | bytes 1048576 | tf_op jit(solution)/shard_map/all_to_all | solution.py:132
  74.5 4.0 all-to-all-start.1
  78.6 11.6 %scatter_custom_fusion.2 = f32[128,512]{0,1:T(8,128)S(1)} fusion(s32[2048]{0:T(1024)S(1)} %bitcast.136, bf16[128,2048]{0,1:T(8,128)(2,1)S(1)} %bitcast.127, f32[]{:T(128)} %constant.50.clone.1), kind=kCustom, calls=%fused_computation.23 | custom fusion | flops 524288 | bytes 786436 | tf_op jit(solution)/shard_map/scatter-add | solution.py:37
  91.0 21.0 %all-to-all-done.1 = bf16[128,32,64]{0,2,1:T(8,128)(2,1)S(1)} async-done(((bf16[128,32,64]{0,2,1:T(8,128)(2,1)}), bf16[128,32,64]{0,2,1:T(8,128)(2,1)S(1)}, u32[]{:S(2)}, u32[]{:S(2)}) %all-to-all-start.1) | async-done | bytes 524320 | tf_op jit(solution)/shard_map/all_to_all | solution.py:131
  112.1 4.3 all-to-all-start.8
  116.4 11.6 %scatter_custom_fusion.1 = f32[128,512]{0,1:T(8,128)S(1)} fusion(s32[2048]{0:T(1024)S(1)} %bitcast.137, bf16[128,2048]{0,1:T(8,128)(2,1)S(1)} %bitcast.126, f32[]{:T(128)} %constant.50.clone.1), kind=kCustom, calls=%fused_computation.25 | custom fusion | flops 524288 | bytes 786436 | tf_op jit(solution)/shard_map/scatter-add | solution.py:37
  128.8 3.7 all-to-all-done.8
  132.6 8.9 %all-to-all-start.2 = ((bf16[32,4,512]{2,1,0:T(4,128)(2,1)}), bf16[32,4,512]{2,1,0:T(4,128)(2,1)S(1)}, u32[]{:S(2)}, u32[]{:S(2)}) async-start(bf16[32,4,512]{2,1,0:T(4,128)(2,1)} %all_to_all.88), calls=%async_computation.2 | async-start | bytes 262144 | tf_op jit(solution)/shard_map/all_to_all | solution.py:138
  144.4 2.9 reshape.249
  147.6 2.7 reshape.250
  150.3 5.8 %copy.88 = bf16[4,16,4,2,16,16]{1,3,5,2,0,4:T(2,128)(2,1)S(1)} copy(bf16[4,16,4,2,16,16]{5,4,3,2,1,0:T(8,128)(2,1)} %reshape.250) | data formatting | bytes 524288 | tf_op jit(solution)/shard_map/reshape | solution.py:61
  156.0 1.5 all_to_all.115
  158.0 2.2 reduce.12
  161.1 6.8 %all-to-all-start.9 = ((bf16[16,2,4096]{2,1,0:T(2,128)(2,1)}), bf16[16,2,4096]{2,1,0:T(2,128)(2,1)}, u32[]{:S(2)}, u32[]{:S(2)}) async-start(bf16[16,2,4096]{2,1,0:T(2,128)(2,1)} %reshape.388), calls=%async_computation.9 | async-start | bytes 524288 | tf_op jit(solution)/shard_map/all_to_all | solution.py:157
  169.2 2.9 reshape.237
  172.3 2.7 reshape.238
  175.1 5.8 %copy.74 = bf16[4,16,4,2,16,16]{1,3,5,2,0,4:T(2,128)(2,1)S(1)} copy(bf16[4,16,4,2,16,16]{5,4,3,2,1,0:T(8,128)(2,1)} %reshape.238) | data formatting | bytes 524288 | tf_op jit(solution)/shard_map/reshape | solution.py:61
  180.8 1.5 all_to_all.113
  182.3 2.2 reduce.13
  185.3 6.7 %all-to-all-start.3 = ((bf16[16,2,4096]{2,1,0:T(2,128)(2,1)}), bf16[16,2,4096]{2,1,0:T(2,128)(2,1)}, u32[]{:S(2)}, u32[]{:S(2)}) async-start(bf16[16,2,4096]{2,1,0:T(2,128)(2,1)} %reshape.384), calls=%async_computation.3 | async-start | bytes 524288 | tf_op jit(solution)/shard_map/all_to_all | solution.py:150
  193.1 2.3 reshape.389
  195.4 1.5 reduce.6
  196.9 1.7 reshape.251
  198.6 3.8 copy.90
  202.4 4.5 %reshape.252 = bf16[256,512]{1,0:T(8,128)(2,1)S(1)} reshape(bf16[4,4,16,2,16,16]{5,4,3,2,1,0:T(8,128)(2,1)} %copy.90) | data formatting | bytes 524288 | tf_op jit(solution)/shard_map/reshape | solution.py:72
  207.6 2.2 reshape.385
  209.8 2.2 reduce.4
  212.0 2.6 reshape.239
  214.6 3.8 copy.76
  218.4 4.6 %reshape.240 = bf16[256,512]{1,0:T(8,128)(2,1)S(1)} reshape(bf16[4,4,16,2,16,16]{5,4,3,2,1,0:T(8,128)(2,1)} %copy.76) | data formatting | bytes 524288 | tf_op jit(solution)/shard_map/reshape | solution.py:72
  223.7 2.9 add_reduce_fusion
  227.6 2.7 reshape.241
  230.3 3.9 copy.106
  234.2 1.5 all_to_all.114
  235.7 2.2 reduce.15
  238.8 6.9 %all-to-all-start.4 = ((bf16[16,2,4096]{2,1,0:T(2,128)(2,1)}), bf16[16,2,4096]{2,1,0:T(2,128)(2,1)}, u32[]{:S(2)}, u32[]{:S(2)}) async-start(bf16[16,2,4096]{2,1,0:T(2,128)(2,1)} %reshape.386), calls=%async_computation.4 | async-start | bytes 524288 | tf_op jit(solution)/shard_map/all_to_all | solution.py:204
  245.7 1.6 pad_maximum_fusion.1
  247.7 2.7 reshape.253
  250.5 3.9 copy.105
  254.4 1.5 all_to_all.116
  255.8 2.2 reduce.14
  258.9 6.7 %all-to-all-start.10 = ((bf16[16,2,4096]{2,1,0:T(2,128)(2,1)}), bf16[16,2,4096]{2,1,0:T(2,128)(2,1)S(1)}, u32[]{:S(2)}, u32[]{:S(2)}) async-start(bf16[16,2,4096]{2,1,0:T(2,128)(2,1)} %reshape.390), calls=%async_computation.10 | async-start | bytes 524288 | tf_op jit(solution)/shard_map/all_to_all | solution.py:211
  265.6 2.2 reshape.387
  267.8 1.5 reduce.5
  269.4 1.7 reshape.242
  271.1 5.4 %copy.80 = bf16[4,16,4,2,16,16]{5,4,3,2,1,0:T(8,128)(2,1)} copy(bf16[4,16,4,2,16,16]{1,3,5,2,0,4:T(2,128)(2,1)S(1)} %bitcast.117) | data formatting | bytes 524288 | tf_op jit(solution)/shard_map/transpose | solution.py:85
  276.4 4.5 %reshape.243 = bf16[256,512]{1,0:T(8,128)(2,1)S(1)} reshape(bf16[4,16,4,2,16,16]{5,4,3,2,1,0:T(8,128)(2,1)} %copy.80) | data formatting | bytes 524288 | tf_op jit(solution)/shard_map/reshape | solution.py:88
  281.2 2.5 reshape.244
  285.5 14.5 %all-to-all-start.5 = ((bf16[32,4,512]{2,1,0:T(4,128)(2,1)}), bf16[32,4,512]{2,1,0:T(4,128)(2,1)S(1)}, u32[]{:S(2)}, u32[]{:S(2)}) async-start(bf16[32,4,512]{2,1,0:T(4,128)(2,1)} %copy.82), calls=%async_computation.5 | async-start | bytes 262144 | tf_op jit(solution)/shard_map/all_to_all | solution.py:230
  300.3 1.5 reduce.7
  301.8 1.7 reshape.254
  303.5 5.4 %copy.93 = bf16[4,16,4,2,16,16]{5,4,3,2,1,0:T(8,128)(2,1)} copy(bf16[4,16,4,2,16,16]{1,3,5,2,0,4:T(2,128)(2,1)S(1)} %bitcast.118) | data formatting | bytes 524288 | tf_op jit(solution)/shard_map/transpose | solution.py:85
  308.9 4.5 %reshape.255 = bf16[256,512]{1,0:T(8,128)(2,1)S(1)} reshape(bf16[4,16,4,2,16,16]{5,4,3,2,1,0:T(8,128)(2,1)} %copy.93) | data formatting | bytes 524288 | tf_op jit(solution)/shard_map/reshape | solution.py:88
  313.7 2.5 reshape.256
  318.0 12.2 %all-to-all-start.11 = ((bf16[32,4,512]{2,1,0:T(4,128)(2,1)}), bf16[32,4,512]{2,1,0:T(4,128)(2,1)S(1)}, u32[]{:S(2)}, u32[]{:S(2)}) async-start(bf16[32,4,512]{2,1,0:T(4,128)(2,1)} %copy.95), calls=%async_computation.11 | async-start | bytes 262144 | tf_op jit(solution)/shard_map/all_to_all | solution.py:237
  331.6 14.4 %all-to-all-done.11 = bf16[32,4,512]{2,1,0:T(4,128)(2,1)S(1)} async-done(((bf16[32,4,512]{2,1,0:T(4,128)(2,1)}), bf16[32,4,512]{2,1,0:T(4,128)(2,1)S(1)}, u32[]{:S(2)}, u32[]{:S(2)}) %all-to-all-start.11) | async-done | bytes 131104 | tf_op jit(solution)/shard_map/all_to_all | solution.py:237
  346.2 6.2 %gather_fusion.2 = bf16[2048,128]{1,0:T(8,128)(2,1)S(1)} fusion(bf16[128,512]{0,1:T(8,128)(2,1)S(1)} %copy.83, s32[2048]{0:T(1024)S(1)} %fusion.21), kind=kCustom, calls=%fused_computation.1.clone | custom fusion | bytes 1056768 | tf_op jit(solution)/shard_map/jit(_take)/gather | solution.py:245
  352.3 6.2 %gather_fusion.5 = bf16[2048,128]{1,0:T(8,128)(2,1)S(1)} fusion(bf16[128,512]{0,1:T(8,128)(2,1)S(1)} %copy.96, s32[2048]{0:T(1024)S(1)} %fusion.21), kind=kCustom, calls=%fused_computation.4.clone | custom fusion | bytes 1056768 | tf_op jit(solution)/shard_map/jit(_take)/gather | solution.py:246
  358.6 1.1 broadcast_select_fusion
  359.7 37.7 %all_to_all.131 = bf16[128,32,64]{0,2,1:T(8,128)(2,1)S(1)} all-to-all(bf16[128,32,64]{0,2,1:T(8,128)(2,1)S(1)} %bitcast.125), channel_id=1, replica_groups=mesh['slab'=16,'row'=32] {'row'}, dimensions={1} | all-to-all | bytes 1048576 | tf_op jit(solution)/shard_map/all_to_all | solution.py:248
  397.4 4.3 all-to-all-start.12
  403.2 32.1 %all-to-all-done.12 = bf16[128,32,64]{0,2,1:T(8,128)(2,1)S(1)} async-done(((bf16[128,32,64]{0,2,1:T(8,128)(2,1)}), bf16[128,32,64]{0,2,1:T(8,128)(2,1)S(1)}, u32[]{:S(2)}, u32[]{:S(2)}) %all-to-all-start.12) | async-done | bytes 524320 | tf_op jit(solution)/shard_map/all_to_all | solution.py:249
  (117 shorter events, 35.1 us)
Async XLA Ops:
  2.2 0.6 copy-start.12
  6.6 28.5 %all-to-all-start = ((s32[32,64,1]{1,2,0:T(1,128)}), s32[32,64,1]{1,2,0:T(1,128)S(1)}, u32[]{:S(2)}, u32[]{:S(2)}) async-start(s32[32,64,1]{1,2,0:T(1,128)} %copy.69), calls=%async_computation | async-start | bytes 32768 | tf_op jit(solution)/shard_map/all_to_all | solution.py:134
  24.0 3.1 copy-start.10
  28.8 87.5 %copy-start.8 = (bf16[4,16,2,256]{3,2,1,0:T(2,128)(2,1)S(1)}, bf16[4,16,2,256]{3,2,1,0:T(2,128)(2,1)}, u32[]{:S(2)}) copy-start(bf16[4,16,2,256]{3,2,1,0:T(2,128)(2,1)} %param.14) | copy-start | bytes 196612
  74.5 37.6 %all-to-all-start.1 = ((bf16[128,32,64]{0,2,1:T(8,128)(2,1)}), bf16[128,32,64]{0,2,1:T(8,128)(2,1)S(1)}, u32[]{:S(2)}, u32[]{:S(2)}) async-start(bf16[128,32,64]{0,2,1:T(8,128)(2,1)} %bitcast.8), calls=%async_computation.1 | async-start | bytes 1048576 | tf_op jit(solution)/shard_map/all_to_all | solution.py:131
  112.1 20.5 %all-to-all-start.8 = ((bf16[32,4,512]{2,1,0:T(4,128)(2,1)}), bf16[32,4,512]{2,1,0:T(4,128)(2,1)S(1)}, u32[]{:S(2)}, u32[]{:S(2)}) async-start(bf16[32,4,512]{2,1,0:T(4,128)(2,1)} %all_to_all.102), calls=%async_computation.8 | async-start | bytes 262144 | tf_op jit(solution)/shard_map/all_to_all | solution.py:139
  132.6 28.5 %all-to-all-start.2 = ((bf16[32,4,512]{2,1,0:T(4,128)(2,1)}), bf16[32,4,512]{2,1,0:T(4,128)(2,1)S(1)}, u32[]{:S(2)}, u32[]{:S(2)}) async-start(bf16[32,4,512]{2,1,0:T(4,128)(2,1)} %all_to_all.88), calls=%async_computation.2 | async-start | bytes 262144 | tf_op jit(solution)/shard_map/all_to_all | solution.py:138
  161.1 24.2 %all-to-all-start.9 = ((bf16[16,2,4096]{2,1,0:T(2,128)(2,1)}), bf16[16,2,4096]{2,1,0:T(2,128)(2,1)}, u32[]{:S(2)}, u32[]{:S(2)}) async-start(bf16[16,2,4096]{2,1,0:T(2,128)(2,1)} %reshape.388), calls=%async_computation.9 | async-start | bytes 524288 | tf_op jit(solution)/shard_map/all_to_all | solution.py:157
  185.3 22.3 %all-to-all-start.3 = ((bf16[16,2,4096]{2,1,0:T(2,128)(2,1)}), bf16[16,2,4096]{2,1,0:T(2,128)(2,1)}, u32[]{:S(2)}, u32[]{:S(2)}) async-start(bf16[16,2,4096]{2,1,0:T(2,128)(2,1)} %reshape.384), calls=%async_computation.3 | async-start | bytes 524288 | tf_op jit(solution)/shard_map/all_to_all | solution.py:150
  193.1 13.8 %copy-start.5 = (bf16[256,256]{1,0:T(8,128)(2,1)}, bf16[256,256]{1,0:T(8,128)(2,1)S(1)}, u32[]{:S(2)}) copy-start(bf16[256,256]{1,0:T(8,128)(2,1)S(1)} %get-tuple-element.44) | copy-start | bytes 393220
  193.1 29.9 %copy-start.2 = (bf16[256,256]{1,0:T(8,128)(2,1)}, bf16[256,256]{1,0:T(8,128)(2,1)S(1)}, u32[]{:S(2)}) copy-start(bf16[256,256]{1,0:T(8,128)(2,1)S(1)} %get-tuple-element.43) | copy-start | bytes 393220
  218.4 4.6 %copy-start.6 = (bf16[256,256]{1,0:T(8,128)(2,1)S(1)}, bf16[256,256]{1,0:T(8,128)(2,1)}, u32[]{:S(2)}) copy-start(bf16[256,256]{1,0:T(8,128)(2,1)} %copy-done.5) | copy-start | bytes 393220
  218.4 5.2 %copy-start = (f32[4,16,256]{2,1,0:T(8,128)S(1)}, f32[4,16,256]{2,1,0:T(8,128)}, u32[]{:S(2)}) copy-start(f32[4,16,256]{2,1,0:T(8,128)} %get-tuple-element.27) | copy-start | bytes 196612
  218.4 5.3 %copy-start.1 = (f32[4,16,256]{2,1,0:T(8,128)S(1)}, f32[4,16,256]{2,1,0:T(8,128)}, u32[]{:S(2)}) copy-start(f32[4,16,256]{2,1,0:T(8,128)} %get-tuple-element.28) | copy-start | bytes 196612
  223.7 3.6 copy-start.3
  235.7 11.7 %copy-start.4 = (bf16[256,256]{1,0:T(8,128)(2,1)S(1)}, bf16[256,256]{1,0:T(8,128)(2,1)}, u32[]{:S(2)}) copy-start(bf16[256,256]{1,0:T(8,128)(2,1)} %copy-done.2) | copy-start | bytes 393220
  235.7 11.7 %copy-start.7 = (bf16[256,256]{1,0:T(8,128)(2,1)S(1)}, bf16[256,256]{1,0:T(8,128)(2,1)}, u32[]{:S(2)}) copy-start(bf16[256,256]{1,0:T(8,128)(2,1)} %copy-done.5) | copy-start | bytes 393220
  238.8 20.1 %all-to-all-start.4 = ((bf16[16,2,4096]{2,1,0:T(2,128)(2,1)}), bf16[16,2,4096]{2,1,0:T(2,128)(2,1)}, u32[]{:S(2)}, u32[]{:S(2)}) async-start(bf16[16,2,4096]{2,1,0:T(2,128)(2,1)} %reshape.386), calls=%async_computation.4 | async-start | bytes 524288 | tf_op jit(solution)/shard_map/all_to_all | solution.py:204
  258.9 26.6 %all-to-all-start.10 = ((bf16[16,2,4096]{2,1,0:T(2,128)(2,1)}), bf16[16,2,4096]{2,1,0:T(2,128)(2,1)S(1)}, u32[]{:S(2)}, u32[]{:S(2)}) async-start(bf16[16,2,4096]{2,1,0:T(2,128)(2,1)} %reshape.390), calls=%async_computation.10 | async-start | bytes 524288 | tf_op jit(solution)/shard_map/all_to_all | solution.py:211
  285.5 32.5 %all-to-all-start.5 = ((bf16[32,4,512]{2,1,0:T(4,128)(2,1)}), bf16[32,4,512]{2,1,0:T(4,128)(2,1)S(1)}, u32[]{:S(2)}, u32[]{:S(2)}) async-start(bf16[32,4,512]{2,1,0:T(4,128)(2,1)} %copy.82), calls=%async_computation.5 | async-start | bytes 262144 | tf_op jit(solution)/shard_map/all_to_all | solution.py:230
  318.0 28.0 %all-to-all-start.11 = ((bf16[32,4,512]{2,1,0:T(4,128)(2,1)}), bf16[32,4,512]{2,1,0:T(4,128)(2,1)S(1)}, u32[]{:S(2)}, u32[]{:S(2)}) async-start(bf16[32,4,512]{2,1,0:T(4,128)(2,1)} %copy.95), calls=%async_computation.11 | async-start | bytes 262144 | tf_op jit(solution)/shard_map/all_to_all | solution.py:237
  358.5 43.2 %copy-start.9 = (s32[32,1]{0,1:T(1,128)S(1)}, s32[32,1]{0,1:T(1,128)}, u32[]{:S(2)}) copy-start(s32[32,1]{0,1:T(1,128)} %param.15) | copy-start | bytes 388
  358.5 43.2 %copy-start.13 = (s32[32]{0:T(128)S(1)}, s32[32]{0:T(128)}, u32[]{:S(2)}) copy-start(s32[32]{0:T(128)} %copy-done.12) | copy-start | bytes 388
  397.4 37.9 %all-to-all-start.12 = ((bf16[128,32,64]{0,2,1:T(8,128)(2,1)}), bf16[128,32,64]{0,2,1:T(8,128)(2,1)S(1)}, u32[]{:S(2)}, u32[]{:S(2)}) async-start(bf16[128,32,64]{0,2,1:T(8,128)(2,1)} %bitcast.40), calls=%async_computation.12 | async-start | bytes 1048576 | tf_op jit(solution)/shard_map/all_to_all | solution.py:249
  403.2 32.8 %copy-start.11 = (pred[1024]{0:T(1024)(128)(4,1)S(1)}, pred[1024]{0:T(1024)(128)(4,1)}, u32[]{:S(2)}) copy-start(pred[1024]{0:T(1024)(128)(4,1)} %copy-done.10) | copy-start | bytes 3076
where the time goes:
time: 446 us; the launch traced here: 438 us
  local copies, waits for them, and re-layouts  135 us (30%)
  starting transfers between devices  92 us (21%)
  waiting for transfers between devices  77.5 us (17%)
  blocking collectives  77.1 us (17%)
  other arithmetic  51.7 us (12%)
    all_to_all x1, blocking collectives, on_device(): lax.all_to_all(pack_slots(cot_live), 'row', split_axis=1, concat_axis=1,...  39.4 us
    all_to_all x1, blocking collectives, on_device(): lax.all_to_all(field_vals, 'row', split_axis=1, concat_axis=1, tiled=True)  37.7 us
    all_to_all x1, waiting for transfers between devices, on_device(): lax.all_to_all(cot_vals, 'row', split_axis=1, concat_axis=1, tiled=True)  32.1 us
    scatter-add x2, other arithmetic, spread(): summed = jnp.zeros((values.shape[0], total_cells), jnp.float32).at[:, cel...  23.1 us
    all_to_all x1, waiting for transfers between devices, on_device(): lax.all_to_all(pack_slots(feats_live), 'row', split_axis=1, concat_axis=1...  21 us
    reshape x4, local copies, waits for them, and re-layouts, to_columns(): rows_in.reshape(chan_local, slab_rows, NY, 2, slab_count, kx_local)  17 us
    all_to_all x1, starting transfers between devices, on_device(): lax.all_to_all(send_offsets, 'row', split_axis=0, concat_axis=0, tiled=True)  16.7 us
    unnamed x43, local copies, waits for them, and re-layouts  15.8 us
  transfers between devices with their start and end apart: 11, of which 5 were waited for; matrix products, arithmetic and copies ran while one was open for 30% of the time, Pallas kernels for 0%

commit v1 on v0

v1 whole, which is shorter than its diff:
```python
import jax
import jax.numpy as jnp
import numpy as np
from jax import lax
from jax.experimental import pallas as pl
from jax.experimental.pallas import tpu as pltpu
from jax.sharding import PartitionSpec as P

C = 128
NX = 256
NZ = 256
NY = 4
BLK = 32
N_SLAB = 16
N_ROW = 32
CL = C // N_ROW
KX = NX // N_SLAB
ZL = NZ // N_SLAB
A_DEV = 1024
LT = A_DEV // 128
ROWS = CL * NY * ZL
INV = 1.0 / (NX * NZ)
BF = jnp.bfloat16
F32 = jnp.float32
NT = (((1,), (1,)), ((), ()))
TN = (((0,), (0,)), ((), ()))
NN = (((1,), (0,)), ((), ()))
VMEM = pl.BlockSpec(memory_space=pltpu.VMEM)
PARAMS = pltpu.CompilerParams(vmem_limit_bytes=24 << 20)


def trig_table(length):
    n = np.arange(length)
    angles = (np.outer(n, n) % length) * (2.0 * np.pi / length)
    return np.cos(angles), np.sin(angles)


def make_tables():
    cos_x, sin_x = trig_table(NX)
    cos_z, sin_z = trig_table(NZ)
    table_x = np.concatenate([cos_x, -sin_x], axis=1)
    upper = np.concatenate([cos_z, -sin_z], axis=1)
    lower = np.concatenate([sin_z, cos_z], axis=1)
    table_z = np.concatenate([upper, lower], axis=0)
    table_z = table_z.reshape(2, N_SLAB, ZL, 2 * NZ).transpose(1, 0, 2, 3).reshape(2 * NZ, 2 * NZ)
    return jnp.asarray(table_x.astype(np.float32)).astype(BF), jnp.asarray(
        table_z.astype(np.float32)
    ).astype(BF)


def swap_chunks(parts):
    parts = list(parts)
    chunk = lax.broadcasted_iota(jnp.int32, parts[0].shape, 1) // KX
    for step in (1, 2, 4):
        upper = (chunk & step) != 0
        for i in range(8):
            if i & step:
                continue
            first, second = parts[i], parts[i | step]
            parts[i] = jnp.where(upper, pltpu.roll(second, step * KX, 1), first)
            parts[i | step] = jnp.where(upper, second, pltpu.roll(first, 128 - step * KX, 1))
    return parts


def encode_cells(cells, live):
    value = 1.0 + (cells & 127).astype(F32) * (1.0 / 128.0)
    for bit in range(6):
        value = value * jnp.where((cells >> (7 + bit)) & 1 == 1, 2.0 ** (1 << bit), 1.0)
    value = value * jnp.where((cells >> 13) & 1 == 1, 1.0, 2.0**-64)
    return jnp.where(live, value, 0.0).astype(BF)


def decode_cells(code):
    value = code.astype(F32)
    live = value > 0.0
    top = value >= 1.0
    value = jnp.where(top, value, value * 2.0**64)
    high = jnp.where(top, 64, 0)
    for bit in range(5, -1, -1):
        over = value >= 2.0 ** (1 << bit)
        value = jnp.where(over, value * 2.0 ** -(1 << bit), value)
        high = high + jnp.where(over, 1 << bit, 0)
    low = ((value - 1.0) * 128.0).astype(jnp.int32)
    return jnp.where(live, high * 128 + low, -1)


def one_hot_x(x_cell, j):
    line = lax.broadcasted_iota(jnp.int32, (NX, 128), 0)
    return jnp.where(jnp.broadcast_to(x_cell[j : j + 1], (NX, 128)) == line, 1.0, 0.0).astype(BF)


def zy_mask(zy_cell, j):
    line = lax.broadcasted_iota(jnp.int32, (NY * ZL, 128), 0)
    return jnp.broadcast_to(zy_cell[j : j + 1], (NY * ZL, 128)) == line


def spread_kernel(scale, value_ref, code_ref, table_ref, out_ref, acc_ref):
    acc_ref[...] = jnp.zeros_like(acc_ref)

    def one_brick(src, carry):
        cells = decode_cells(code_ref[src, CL * LT : (CL + 1) * LT, :])
        zy_cell, x_cell = cells >> 8, cells & (NX - 1)
        values = value_ref[src, 0 : CL * LT, :].astype(F32)
        left, right = [], []
        for j in range(LT):
            mask = zy_mask(zy_cell, j)
            right.append(one_hot_x(x_cell, j))
            left.append(
                jnp.concatenate(
                    [
                        jnp.where(
                            mask,
                            jnp.broadcast_to(values[c * LT + j : c * LT + j + 1], mask.shape),
                            0.0,
                        ).astype(BF)
                        for c in range(CL)
                    ],
                    axis=0,
                )
            )
        acc_ref[...] += lax.dot_general(
            jnp.concatenate(left, axis=1),
            jnp.concatenate(right, axis=1),
            NT,
            preferred_element_type=F32,
        )
        return carry

    lax.fori_loop(0, N_ROW, one_brick, 0)
    rows = jnp.dot(acc_ref[...].astype(BF), table_ref[...], preferred_element_type=F32)
    if scale != 1.0:
        rows = rows * scale
    for part in range(2):
        for group in range(CL * NY // 8):
            for half in range(2):
                lanes = part * NX + half * 128
                chunks = swap_chunks(
                    [
                        rows[(group * 8 + i) * ZL : (group * 8 + i + 1) * ZL, lanes : lanes + 128]
                        for i in range(8)
                    ]
                )
                for j in range(8):
                    out_ref[
                        half * 8 + j, part * ZL : (part + 1) * ZL, group * 128 : (group + 1) * 128
                    ] = chunks[j].astype(BF)


def spread(values, codes, table_x, scale):
    return pl.pallas_call(
        lambda *refs: spread_kernel(scale, *refs),
        out_shape=jax.ShapeDtypeStruct((N_SLAB, 2 * ZL, CL * NY * KX), BF),
        in_specs=[VMEM] * 3,
        out_specs=VMEM,
        scratch_shapes=[pltpu.VMEM((ROWS, NX), F32)],
        compiler_params=PARAMS,
        name="spread",
    )(values, codes, table_x)


def spectral_kernel(feat_ref, cot_ref, table_ref, filter_ref, out_f_ref, out_c_ref, grad_ref):
    table = table_ref[...]
    lines = CL * NY * KX

    def to_modes(ref):
        flat = ref[...].reshape(2 * NZ, lines)
        return lax.dot_general(flat, table, TN, preferred_element_type=F32).astype(BF).astype(F32)

    spec, cot = to_modes(feat_ref), to_modes(cot_ref)
    filtered, cot_spec = [], []
    for c in range(CL):
        filt = filter_ref[c * KX : (c + 1) * KX, :].astype(F32)
        fr, fi = filt[:, :NZ], filt[:, NZ:]
        grad_r = jnp.zeros((KX, NZ), F32)
        grad_i = jnp.zeros((KX, NZ), F32)
        for y in range(NY):
            rows = slice((c * NY + y) * KX, (c * NY + y + 1) * KX)
            sr, si = spec[rows, :NZ], spec[rows, NZ:]
            gr, gi = cot[rows, :NZ], cot[rows, NZ:]
            filtered.append(jnp.concatenate([sr * fr - si * fi, sr * fi + si * fr], axis=1).astype(BF))
            cot_spec.append(jnp.concatenate([gr * fr + gi * fi, gi * fr - gr * fi], axis=1).astype(BF))
            grad_r = grad_r + (gr * sr + gi * si)
            grad_i = grad_i + (gi * sr - gr * si)
        grad_ref[c * KX : (c + 1) * KX, :NZ] = grad_r
        grad_ref[c * KX : (c + 1) * KX, NZ:] = grad_i
    for parts, ref in ((filtered, out_f_ref), (cot_spec, out_c_ref)):
        planes = lax.dot_general(
            table, jnp.concatenate(parts, axis=0), NT, preferred_element_type=F32
        )
        ref[...] = planes.astype(BF).reshape(ref.shape)


def spectral(feat_cols, cot_cols, table_z, filters):
    shape = jax.ShapeDtypeStruct((N_SLAB, 2 * ZL, CL * NY * KX), BF)
    return pl.pallas_call(
        spectral_kernel,
        out_shape=(shape, shape, jax.ShapeDtypeStruct((CL * KX, 2 * NZ), F32)),
        in_specs=[VMEM] * 4,
        out_specs=(VMEM,) * 3,
        compiler_params=PARAMS,
        name="spectral",
    )(feat_cols, cot_cols, table_z, filters)


def gather_kernel(scale, plane_ref, code_ref, table_ref, out_ref, rows_ref):
    for part in range(2):
        for group in range(CL * NY // 8):
            for half in range(2):
                chunks = swap_chunks(
                    [
                        plane_ref[
                            half * 8 + j,
                            part * ZL : (part + 1) * ZL,
                            group * 128 : (group + 1) * 128,
                        ].astype(F32)
                        for j in range(8)
                    ]
                )
                lanes = part * NX + half * 128
                for i in range(8):
                    rows_ref[
                        (group * 8 + i) * ZL : (group * 8 + i + 1) * ZL, lanes : lanes + 128
                    ] = chunks[i].astype(BF)
    field = lax.dot_general(rows_ref[...], table_ref[...], NT, preferred_element_type=F32)
    if scale != 1.0:
        field = field * scale
    field = field.astype(BF)
    sub = lax.broadcasted_iota(jnp.int32, (LT, 128), 0)

    def one_brick(src, carry):
        cells = decode_cells(code_ref[src, CL * LT : (CL + 1) * LT, :])
        zy_cell, x_cell = cells >> 8, cells & (NX - 1)
        picks = jnp.concatenate([one_hot_x(x_cell, j) for j in range(LT)], axis=1)
        lines = jnp.dot(field, picks, preferred_element_type=F32)
        found = [jnp.zeros((LT, 128), F32) for _ in range(CL)]
        for j in range(LT):
            mask = zy_mask(zy_cell, j)
            for c in range(CL):
                line = lines[c * NY * ZL : (c + 1) * NY * ZL, j * 128 : (j + 1) * 128]
                total = jnp.sum(jnp.where(mask, line, 0.0), axis=0, keepdims=True)
                found[c] = jnp.where(sub == j, jnp.broadcast_to(total, (LT, 128)), found[c])
        out_ref[src] = jnp.concatenate(found, axis=0).astype(BF)
        return carry

    lax.fori_loop(0, N_ROW, one_brick, 0)


def gather(planes, codes, table_x, scale):
    return pl.pallas_call(
        lambda *refs: gather_kernel(scale, *refs),
        out_shape=jax.ShapeDtypeStruct((N_ROW, CL * LT, 128), BF),
        in_specs=[VMEM] * 3,
        out_specs=VMEM,
        scratch_shapes=[pltpu.VMEM((ROWS, 2 * NX), BF)],
        compiler_params=PARAMS,
        name="gather",
    )(planes, codes, table_x)


def atom_codes(block_tiles, cell_offsets, live_counts):
    slot = jnp.arange(A_DEV, dtype=jnp.int32)
    tile = jnp.broadcast_to(block_tiles, (A_DEV // BLK, BLK)).reshape(A_DEV)
    offset = cell_offsets
    zy_cell = ((offset >> 3) & (NY - 1)) * ZL + (offset >> 5)
    cells = zy_cell * NX + tile * (NX // N_ROW) + (offset & 7)
    return encode_cells(cells, slot < live_counts[0])


def on_device(atom_feats, cotangent, filter_modes, block_tiles, cell_offsets, live_counts):
    table_x, table_z = make_tables()
    code = atom_codes(block_tiles, cell_offsets, live_counts).reshape(1, LT, 128)
    feats = jnp.concatenate(
        [
            atom_feats.reshape(N_ROW, CL * LT, 128),
            jnp.broadcast_to(code, (N_ROW, LT, 128)),
        ],
        axis=1,
    )
    cots = cotangent.reshape(N_ROW, CL * LT, 128)

    def over(axis, values):
        return lax.all_to_all(values, axis, split_axis=0, concat_axis=0, tiled=True)

    got_feats = over("row", feats)
    got_cots = over("row", cots)
    feat_cols = over("slab", spread(got_feats, got_feats, table_x, 1.0))
    cot_cols = over("slab", spread(got_cots, got_feats, table_x, INV))
    filters = filter_modes.reshape(CL * KX, 2 * NZ)
    planes, cot_planes, grad = spectral(feat_cols, cot_cols, table_z, filters)
    field_vals = gather(over("slab", planes), got_feats, table_x, INV)
    cot_vals = gather(over("slab", cot_planes), got_feats, table_x, 1.0)
    long_range = over("row", field_vals).reshape(C, A_DEV)
    grad_feats = over("row", cot_vals).reshape(C, A_DEV)
    return (long_range, grad_feats, grad.reshape(CL, KX, 2, NZ))


def solution(mesh):
    in_specs = (
        P(None, ("slab", "row")),
        P(None, ("slab", "row")),
        P("row", "slab", None, None),
        P(("slab", "row"), None),
        P(("slab", "row")),
        P(("slab", "row")),
    )
    out_specs = (P(None, ("slab", "row")), P(None, ("slab", "row")), P("row", "slab", None, None))
    return jax.shard_map(
        on_device, mesh=mesh, in_specs=in_specs, out_specs=out_specs, check_vma=False
    )
```

time: 446 us -> 194 us (0.43); the launches traced: 438 us -> 192 us
  local copies, waits for them, and re-layouts: 135 us -> 4.46 us
  blocking collectives: 77.1 us -> 10.4 us
  Pallas kernels: 0 us -> 55.9 us
  other arithmetic: 51.7 us -> 0.79 us
  starting transfers between devices: 92 us -> 51.3 us
  waiting for transfers between devices: 77.5 us -> 67.9 us
    all_to_all x2 -> x1, blocking collectives: 77.1 us -> 10.4 us  [over(): return lax.all_to_all(values, axis, split_axis=0, concat_axis=0, tiled=True)]
    reshape x21 -> x5, local copies, waits for them, and re-layouts: 67.5 us -> 4.27 us  [the longest x1 1.08 us: on_device(): atom_feats.reshape(N_ROW, CL * LT, 128)]
    pallas_call x0 -> x5, Pallas kernels: none -> 55.9 us  [the longest x2 27.2 us: gather(): pl.pallas_call(lambda *refs: gather_kernel(scale, *refs), out_shape=jax.S...]
    all_to_all x11 -> x7, starting transfers between devices: 92 us -> 51.3 us  [over(): return lax.all_to_all(values, axis, split_axis=0, concat_axis=0, tiled=True)]
    scatter-add x2 -> x0, other arithmetic: 23.1 us -> none  [spread(): summed = jnp.zeros((values.shape[0], total_cells), jnp.float32).at[:, cel...]
    transpose x8 -> x0, local copies, waits for them, and re-layouts: 22.1 us -> none  [the longest x2 10.7 us: from_planes(): received.reshape(slab_count, chan_local, NY, kx_local, 2, slab_rows)]
    all_to_all x9 -> x0, other arithmetic: 16.1 us -> none  [the longest x2 4.38 us: on_device(): lax.all_to_all(to_columns(row_feats, slab_count, slab_rows), 'slab', spli...]
    unnamed x43 -> x13, local copies, waits for them, and re-layouts: 15.8 us -> 0.04 us
  transfers between devices with their start and end apart: 11 -> 7, of which waited for: 5 -> 5; matrix products, arithmetic and copies ran while one was open for 30% -> 1% of each run, Pallas kernels for 0% -> 28%
where the time goes in v1:
time: 194 us; the launch traced here: 192 us
  waiting for transfers between devices  67.9 us (35%)
  Pallas kernels  55.9 us (29%)
  starting transfers between devices  51.3 us (26%)
  blocking collectives  10.4 us (5%)
  local copies, waits for them, and re-layouts  4.46 us (2%)
    all_to_all x7, waiting for transfers between devices, over(): return lax.all_to_all(values, axis, split_axis=0, concat_axis=0, tiled=True)  67.9 us
    all_to_all x7, starting transfers between devices, over(): return lax.all_to_all(values, axis, split_axis=0, concat_axis=0, tiled=True)  51.3 us
    pallas_call x2, Pallas kernels, gather(): pl.pallas_call(lambda *refs: gather_kernel(scale, *refs), out_shape=jax.S...  27.2 us
    pallas_call x2, Pallas kernels, spread(): pl.pallas_call(lambda *refs: spread_kernel(scale, *refs), out_shape=jax.S...  27.1 us
    all_to_all x1, blocking collectives, over(): return lax.all_to_all(values, axis, split_axis=0, concat_axis=0, tiled=True)  10.4 us
  transfers between devices with their start and end apart: 7, of which 5 were waited for; matrix products, arithmetic and copies ran while one was open for 1% of the time, Pallas kernels for 28%

profile of v1, /device:TPU:1, one launch (start us, length us, event | category | flops | bytes accessed | tf_op | source)
XLA Modules:
  0.0 192.3 jit_solution(7687260157516698947)
XLA Ops:
  0.6 0.0 copy-start.5
  1.3 0.0 copy-done.5
  1.3 0.1 broadcast_in_dim.46
  1.4 0.1 mul.55
  1.5 0.0 copy-start.4
  1.5 1.1 reshape.31
  2.6 0.0 copy-done.4
  2.6 0.8 pad_maximum_fusion
  3.4 0.0 copy-start.2
  3.4 16.9 %all-to-all-start = ((bf16[32,40,128]{2,1,0:T(8,128)(2,1)}), bf16[32,40,128]{2,1,0:T(8,128)(2,1)S(1)}, u32[]{:S(2)}, u32[]{:S(2)}) async-start(bf16[32,40,128]{2,1,0:T(8,128)(2,1)} %pad_maximum_fusion), calls=%async_computation | async-start | bytes 655360 | tf_op jit(solution)/shard_map/all_to_all | solution.py:282
  20.2 0.0 copy-done.2
  20.3 0.8 reshape.32
  21.1 0.0 copy-start
  21.1 24.2 %all-to-all-done.refs_0_.refs_1_ = bf16[32,40,128]{2,1,0:T(8,128)(2,1)S(1)} async-done(((bf16[32,40,128]{2,1,0:T(8,128)(2,1)}), bf16[32,40,128]{2,1,0:T(8,128)(2,1)S(1)}, u32[]{:S(2)}, u32[]{:S(2)}) %all-to-all-start) | async-done | bytes 327712 | tf_op jit(solution)/shard_map/all_to_all | solution.py:282
  45.2 4.2 %all-to-all-start.2 = ((bf16[32,32,128]{2,1,0:T(8,128)(2,1)}), bf16[32,32,128]{2,1,0:T(8,128)(2,1)S(1)}, u32[]{:S(2)}, u32[]{:S(2)}) async-start(bf16[32,32,128]{2,1,0:T(8,128)(2,1)} %reshape.32), calls=%async_computation.2 | async-start | bytes 524288 | tf_op jit(solution)/shard_map/all_to_all | solution.py:282
  49.5 0.0 copy-done
  49.5 13.6 %spread.2 = bf16[16,32,256]{2,1,0:T(8,128)(2,1)} custom-call(bf16[32,40,128]{2,1,0:T(8,128)(2,1)S(1)} %all-to-all-done.refs_0_.refs_1_, bf16[32,40,128]{2,1,0:T(8,128)(2,1)S(1)} %all-to-all-done.refs_0_.refs_1_, bf16[256,512]{1,0:T(8,128)(2,1)S(1)} %copy-done), custom_call_target="tpu_custom_call" | custom-call | tf_op jit(solution)/shard_map/spread/pallas_call | solution.py:150
  63.1 8.1 %all-to-all-done.2.refs_0_ = bf16[32,32,128]{2,1,0:T(8,128)(2,1)S(1)} async-done(((bf16[32,32,128]{2,1,0:T(8,128)(2,1)}), bf16[32,32,128]{2,1,0:T(8,128)(2,1)S(1)}, u32[]{:S(2)}, u32[]{:S(2)}) %all-to-all-start.2) | async-done | bytes 262176 | tf_op jit(solution)/shard_map/all_to_all | solution.py:282
  71.1 6.8 %all-to-all-start.1 = ((bf16[16,32,256]{2,1,0:T(8,128)(2,1)}), bf16[16,32,256]{2,1,0:T(8,128)(2,1)S(1)}, u32[]{:S(2)}, u32[]{:S(2)}) async-start(bf16[16,32,256]{2,1,0:T(8,128)(2,1)} %spread.2), calls=%async_computation.1 | async-start | bytes 524288 | tf_op jit(solution)/shard_map/all_to_all | solution.py:282
  77.9 0.0 copy-start.3
  77.9 13.6 %spread.3 = bf16[16,32,256]{2,1,0:T(8,128)(2,1)} custom-call(bf16[32,32,128]{2,1,0:T(8,128)(2,1)S(1)} %all-to-all-done.2.refs_0_, bf16[32,40,128]{2,1,0:T(8,128)(2,1)S(1)} %all-to-all-done.refs_0_.refs_1_, bf16[256,512]{1,0:T(8,128)(2,1)S(1)} %copy-done), custom_call_target="tpu_custom_call" | custom-call | tf_op jit(solution)/shard_map/spread/pallas_call | solution.py:150
  91.5 0.0 copy-start.1
  91.5 0.0 all-to-all-done.1.feat_ref
  91.5 6.8 %all-to-all-start.3 = ((bf16[16,32,256]{2,1,0:T(8,128)(2,1)}), bf16[16,32,256]{2,1,0:T(8,128)(2,1)S(1)}, u32[]{:S(2)}, u32[]{:S(2)}) async-start(bf16[16,32,256]{2,1,0:T(8,128)(2,1)} %spread.3), calls=%async_computation.3 | async-start | bytes 524288 | tf_op jit(solution)/shard_map/all_to_all | solution.py:282
  98.3 0.0 copy-done.3
  98.3 7.5 %all-to-all-done.3.cot_ref = bf16[16,32,256]{2,1,0:T(8,128)(2,1)S(1)} async-done(((bf16[16,32,256]{2,1,0:T(8,128)(2,1)}), bf16[16,32,256]{2,1,0:T(8,128)(2,1)S(1)}, u32[]{:S(2)}, u32[]{:S(2)}) %all-to-all-start.3) | async-done | bytes 262176 | tf_op jit(solution)/shard_map/all_to_all | solution.py:282
  105.8 0.0 copy-done.1
  105.8 1.6 spectral.1
  107.4 10.4 %all_to_all.40.refs_0_ = bf16[16,32,256]{2,1,0:T(8,128)(2,1)S(1)} all-to-all(bf16[16,32,256]{2,1,0:T(8,128)(2,1)S(1)} %get-tuple-element.6), channel_id=1, replica_groups=mesh['slab'=16,'row'=32] {'slab'}, dimensions={0} | all-to-all | bytes 524288 | tf_op jit(solution)/shard_map/all_to_all | solution.py:282
  117.9 3.5 %all-to-all-start.6 = ((bf16[16,32,256]{2,1,0:T(8,128)(2,1)}), bf16[16,32,256]{2,1,0:T(8,128)(2,1)S(1)}, u32[]{:S(2)}, u32[]{:S(2)}) async-start(bf16[16,32,256]{2,1,0:T(8,128)(2,1)} %get-tuple-element.7), calls=%async_computation.6 | async-start | bytes 524288 | tf_op jit(solution)/shard_map/all_to_all | solution.py:282
  121.4 13.6 %gather.2 = bf16[32,32,128]{2,1,0:T(8,128)(2,1)} custom-call(bf16[16,32,256]{2,1,0:T(8,128)(2,1)S(1)} %all_to_all.40.refs_0_, bf16[32,40,128]{2,1,0:T(8,128)(2,1)S(1)} %all-to-all-done.refs_0_.refs_1_, bf16[256,512]{1,0:T(8,128)(2,1)S(1)} %copy-done), custom_call_target="tpu_custom_call" | custom-call | tf_op jit(solution)/shard_map/gather/pallas_call | solution.py:249
  135.0 0.0 all-to-all-done.6.refs_0_
  135.0 8.1 %all-to-all-start.5 = ((bf16[32,32,128]{2,1,0:T(8,128)(2,1)}), bf16[32,32,128]{2,1,0:T(8,128)(2,1)S(1)}, u32[]{:S(2)}, u32[]{:S(2)}) async-start(bf16[32,32,128]{2,1,0:T(8,128)(2,1)} %gather.2), calls=%async_computation.5 | async-start | bytes 524288 | tf_op jit(solution)/shard_map/all_to_all | solution.py:282
  143.2 13.6 %gather.3 = bf16[32,32,128]{2,1,0:T(8,128)(2,1)} custom-call(bf16[16,32,256]{2,1,0:T(8,128)(2,1)S(1)} %all-to-all-done.6.refs_0_, bf16[32,40,128]{2,1,0:T(8,128)(2,1)S(1)} %all-to-all-done.refs_0_.refs_1_, bf16[256,512]{1,0:T(8,128)(2,1)S(1)} %copy-done), custom_call_target="tpu_custom_call" | custom-call | tf_op jit(solution)/shard_map/gather/pallas_call | solution.py:249
  156.7 8.1 %all-to-all-done.5 = bf16[32,32,128]{2,1,0:T(8,128)(2,1)S(1)} async-done(((bf16[32,32,128]{2,1,0:T(8,128)(2,1)}), bf16[32,32,128]{2,1,0:T(8,128)(2,1)S(1)}, u32[]{:S(2)}, u32[]{:S(2)}) %all-to-all-start.5) | async-done | bytes 262176 | tf_op jit(solution)/shard_map/all_to_all | solution.py:282
  164.8 5.0 %all-to-all-start.7 = ((bf16[32,32,128]{2,1,0:T(8,128)(2,1)}), bf16[32,32,128]{2,1,0:T(8,128)(2,1)S(1)}, u32[]{:S(2)}, u32[]{:S(2)}) async-start(bf16[32,32,128]{2,1,0:T(8,128)(2,1)} %gather.3), calls=%async_computation.7 | async-start | bytes 524288 | tf_op jit(solution)/shard_map/all_to_all | solution.py:282
  169.8 0.7 reshape.36
  170.6 0.8 reshape.34
  171.4 20.1 %all-to-all-done.7 = bf16[32,32,128]{2,1,0:T(8,128)(2,1)S(1)} async-done(((bf16[32,32,128]{2,1,0:T(8,128)(2,1)}), bf16[32,32,128]{2,1,0:T(8,128)(2,1)S(1)}, u32[]{:S(2)}, u32[]{:S(2)}) %all-to-all-start.7) | async-done | bytes 262176 | tf_op jit(solution)/shard_map/all_to_all | solution.py:282
  191.5 0.8 reshape.35
  (4 shorter events, 0.1 us)
Async XLA Ops:
  0.6 0.7 copy-start.5
  1.5 1.1 copy-start.4
  3.4 16.9 %copy-start.2 = (bf16[128,1024]{1,0:T(8,128)(2,1)S(1)}, bf16[128,1024]{1,0:T(8,128)(2,1)}, u32[]{:S(2)}) copy-start(bf16[128,1024]{1,0:T(8,128)(2,1)} %param.9) | copy-start | bytes 786436
  3.4 41.9 %all-to-all-start = ((bf16[32,40,128]{2,1,0:T(8,128)(2,1)}), bf16[32,40,128]{2,1,0:T(8,128)(2,1)S(1)}, u32[]{:S(2)}, u32[]{:S(2)}) async-start(bf16[32,40,128]{2,1,0:T(8,128)(2,1)} %pad_maximum_fusion), calls=%async_computation | async-start | bytes 655360 | tf_op jit(solution)/shard_map/all_to_all | solution.py:282
  21.1 28.4 %copy-start = (bf16[256,512]{1,0:T(8,128)(2,1)S(1)}, bf16[256,512]{1,0:T(8,128)(2,1)}, u32[]{:S(2)}) copy-start(bf16[256,512]{1,0:T(8,128)(2,1)} %constant.56.refs_2_) | copy-start | bytes 786436
  45.2 25.9 %all-to-all-start.2 = ((bf16[32,32,128]{2,1,0:T(8,128)(2,1)}), bf16[32,32,128]{2,1,0:T(8,128)(2,1)S(1)}, u32[]{:S(2)}, u32[]{:S(2)}) async-start(bf16[32,32,128]{2,1,0:T(8,128)(2,1)} %reshape.32), calls=%async_computation.2 | async-start | bytes 524288 | tf_op jit(solution)/shard_map/all_to_all | solution.py:282
  71.1 20.4 %all-to-all-start.1 = ((bf16[16,32,256]{2,1,0:T(8,128)(2,1)}), bf16[16,32,256]{2,1,0:T(8,128)(2,1)S(1)}, u32[]{:S(2)}, u32[]{:S(2)}) async-start(bf16[16,32,256]{2,1,0:T(8,128)(2,1)} %spread.2), calls=%async_computation.1 | async-start | bytes 524288 | tf_op jit(solution)/shard_map/all_to_all | solution.py:282
  77.9 20.4 %copy-start.3 = (bf16[4,16,2,256]{3,2,1,0:T(2,128)(2,1)S(1)}, bf16[4,16,2,256]{3,2,1,0:T(2,128)(2,1)}, u32[]{:S(2)}) copy-start(bf16[4,16,2,256]{3,2,1,0:T(2,128)(2,1)} %param.10) | copy-start | bytes 196612
  91.5 14.3 %copy-start.1 = (bf16[512,512]{1,0:T(8,128)(2,1)S(1)}, bf16[512,512]{1,0:T(8,128)(2,1)}, u32[]{:S(2)}) copy-start(bf16[512,512]{1,0:T(8,128)(2,1)} %constant.57.table_ref) | copy-start | bytes 1572868
  91.5 14.3 %all-to-all-start.3 = ((bf16[16,32,256]{2,1,0:T(8,128)(2,1)}), bf16[16,32,256]{2,1,0:T(8,128)(2,1)S(1)}, u32[]{:S(2)}, u32[]{:S(2)}) async-start(bf16[16,32,256]{2,1,0:T(8,128)(2,1)} %spread.3), calls=%async_computation.3 | async-start | bytes 524288 | tf_op jit(solution)/shard_map/all_to_all | solution.py:282
  117.9 17.1 %all-to-all-start.6 = ((bf16[16,32,256]{2,1,0:T(8,128)(2,1)}), bf16[16,32,256]{2,1,0:T(8,128)(2,1)S(1)}, u32[]{:S(2)}, u32[]{:S(2)}) async-start(bf16[16,32,256]{2,1,0:T(8,128)(2,1)} %get-tuple-element.7), calls=%async_computation.6 | async-start | bytes 524288 | tf_op jit(solution)/shard_map/all_to_all | solution.py:282
  135.0 29.8 %all-to-all-start.5 = ((bf16[32,32,128]{2,1,0:T(8,128)(2,1)}), bf16[32,32,128]{2,1,0:T(8,128)(2,1)S(1)}, u32[]{:S(2)}, u32[]{:S(2)}) async-start(bf16[32,32,128]{2,1,0:T(8,128)(2,1)} %gather.2), calls=%async_computation.5 | async-start | bytes 524288 | tf_op jit(solution)/shard_map/all_to_all | solution.py:282
  164.8 26.7 %all-to-all-start.7 = ((bf16[32,32,128]{2,1,0:T(8,128)(2,1)}), bf16[32,32,128]{2,1,0:T(8,128)(2,1)S(1)}, u32[]{:S(2)}, u32[]{:S(2)}) async-start(bf16[32,32,128]{2,1,0:T(8,128)(2,1)} %gather.3), calls=%async_computation.7 | async-start | bytes 524288 | tf_op jit(solution)/shard_map/all_to_all | solution.py:282

commit v2 on v1

v2 whole, which is shorter than its diff:
```python
import jax
import jax.numpy as jnp
import numpy as np
from jax import lax
from jax.experimental import pallas as pl
from jax.experimental.pallas import tpu as pltpu
from jax.sharding import PartitionSpec as P

C = 128
NX = 256
NZ = 256
NY = 4
BLK = 32
N_SLAB = 16
N_ROW = 32
CL = C // N_ROW
FC = 2 * CL
KX = NX // N_SLAB
ZL = NZ // N_SLAB
A_DEV = 1024
LT = A_DEV // 128
BLOCKS = A_DEV // BLK
ZY = NY * ZL
HALF = CL * ZY
LINES = CL * NY * KX
INV = 1.0 / (NX * NZ)
PACK = 16
ROWS = N_ROW * LT
GROUP = 16
LIST = ROWS + GROUP + LT
BF = jnp.bfloat16
F32 = jnp.float32
NT = (((1,), (1,)), ((), ()))
TN = (((0,), (0,)), ((), ()))
VMEM = pl.BlockSpec(memory_space=pltpu.VMEM)
SMEM = pl.BlockSpec(memory_space=pltpu.SMEM)
PARAMS = pltpu.CompilerParams(vmem_limit_bytes=32 << 20)


def trig_table(length):
    n = np.arange(length)
    angles = (np.outer(n, n) % length) * (2.0 * np.pi / length)
    return np.cos(angles), np.sin(angles)


def make_tables():
    cos_x, sin_x = trig_table(NX)
    cos_z, sin_z = trig_table(NZ)
    table_x = np.concatenate([cos_x, -sin_x], axis=1)
    upper = np.concatenate([cos_z, -sin_z], axis=1)
    lower = np.concatenate([sin_z, cos_z], axis=1)
    table_z = np.concatenate([upper, lower], axis=0)
    table_z = table_z.reshape(2, N_SLAB, ZL, 2 * NZ).transpose(1, 0, 2, 3).reshape(2 * NZ, 2 * NZ)
    return jnp.asarray(table_x.astype(np.float32)).astype(BF), jnp.asarray(
        table_z.astype(np.float32)
    ).astype(BF)


def swap_chunks(parts):
    parts = list(parts)
    chunk = lax.broadcasted_iota(jnp.int32, parts[0].shape, 1) // KX
    for step in (1, 2, 4):
        upper = (chunk & step) != 0
        for i in range(8):
            if i & step:
                continue
            first, second = parts[i], parts[i | step]
            parts[i] = jnp.where(upper, pltpu.roll(second, step * KX, 1), first)
            parts[i | step] = jnp.where(upper, second, pltpu.roll(first, 128 - step * KX, 1))
    return parts


def encode_cells(cells, live):
    value = 1.0 + (cells & 127).astype(F32) * (1.0 / 128.0)
    for bit in range(6):
        value = value * jnp.where((cells >> (7 + bit)) & 1 == 1, F32(2.0 ** (1 << bit)), F32(1.0))
    value = value * jnp.where((cells >> 13) & 1 == 1, F32(1.0), F32(2.0**-64))
    return jnp.where(live, value, 0.0).astype(BF)


def decode_cells(code):
    value = code.astype(F32)
    live = value > 0.0
    top = value >= 1.0
    value = jnp.where(top, value, value * 2.0**64)
    high = jnp.where(top, 64, 0)
    for bit in range(5, -1, -1):
        over = value >= 2.0 ** (1 << bit)
        value = jnp.where(over, value * 2.0 ** -(1 << bit), value)
        high = high + jnp.where(over, 1 << bit, 0)
    low = ((value - 1.0) * 128.0).astype(jnp.int32)
    return jnp.where(live, high * 128 + low, -1)


def pack_kernel(tile_ref, live_ref, feat_ref, cot_ref, offset_ref, out_ref):
    shape = (LT, 128)
    slot = lax.broadcasted_iota(jnp.int32, shape, 0) * 128 + lax.broadcasted_iota(
        jnp.int32, shape, 1
    )
    block = slot // BLK
    tile = jnp.zeros(shape, jnp.int32)
    for n in range(BLOCKS):
        tile = jnp.where(block == n, tile_ref[n], tile)
    offset = offset_ref[...]
    zy_cell = ((offset >> 3) & (NY - 1)) * ZL + (offset >> 5)
    cells = zy_cell * NX + tile * (NX // N_ROW) + (offset & 7)
    code = encode_cells(cells, slot < live_ref[0])
    low = lax.broadcasted_iota(jnp.int32, (FC, 128), 0) < CL
    for j in range(LT):
        lanes = slice(j * 128, (j + 1) * 128)
        for pair in range(N_ROW // 2):
            rows = slice(pair * FC, (pair + 1) * FC)
            feat = feat_ref[rows, lanes].astype(F32)
            cot = cot_ref[rows, lanes].astype(F32)
            out_ref[2 * pair, j] = jnp.where(low, feat, pltpu.roll(cot, CL, 0)).astype(BF)
            out_ref[2 * pair + 1, j] = jnp.where(low, pltpu.roll(feat, CL, 0), cot).astype(BF)
    for owner in range(N_ROW):
        out_ref[owner, LT] = code


def pack(atom_feats, cotangent, block_tiles, cell_offsets, live_counts):
    return pl.pallas_call(
        pack_kernel,
        out_shape=jax.ShapeDtypeStruct((N_ROW, LT + 1, FC, 128), BF),
        in_specs=[SMEM, SMEM, VMEM, VMEM, VMEM],
        out_specs=VMEM,
        compiler_params=PARAMS,
        name="pack",
    )(
        block_tiles.reshape(BLOCKS),
        live_counts,
        atom_feats,
        cotangent,
        cell_offsets.reshape(LT, 128),
    )


def unpack_kernel(in_ref, feat_ref, cot_ref):
    low = lax.broadcasted_iota(jnp.int32, (FC, 128), 0) < CL
    for j in range(LT):
        lanes = slice(j * 128, (j + 1) * 128)
        for pair in range(N_ROW // 2):
            rows = slice(pair * FC, (pair + 1) * FC)
            first = in_ref[2 * pair, j].astype(F32)
            second = in_ref[2 * pair + 1, j].astype(F32)
            feat_ref[rows, lanes] = jnp.where(low, first, pltpu.roll(second, CL, 0)).astype(BF)
            cot_ref[rows, lanes] = jnp.where(low, pltpu.roll(first, CL, 0), second).astype(BF)


def unpack(values):
    shape = jax.ShapeDtypeStruct((C, A_DEV), BF)
    return pl.pallas_call(
        unpack_kernel,
        out_shape=(shape, shape),
        in_specs=[VMEM],
        out_specs=(VMEM, VMEM),
        compiler_params=PARAMS,
        name="unpack",
    )(values)


def on_rows(row, dtype):
    return jnp.broadcast_to(row, (PACK, 128)).astype(dtype)


def line_numbers(count, dtype):
    return [
        (lax.broadcasted_iota(jnp.int32, (PACK, 128), 0) + first).astype(F32).astype(dtype)
        for first in range(0, count, PACK)
    ]


def one_hot_x(x_row, lines):
    cell = on_rows(x_row, BF)
    one, zero = jnp.ones((PACK, 128), BF), jnp.zeros((PACK, 128), BF)
    return jnp.concatenate([jnp.where(cell == line, one, zero) for line in lines], axis=0)


def sum_rows(blocks):
    sub = lax.broadcasted_iota(jnp.int32, (8, 128), 0)
    low = (sub & 4) == 0
    blocks = [
        jnp.where(low, first, second) + pltpu.roll(jnp.where(low, second, first), 4, 0)
        for first, second in zip(blocks[:4], blocks[4:])
    ]
    for step in (2, 1):
        low = (sub & step) == 0
        blocks = [
            jnp.where(low, first + pltpu.roll(first, 8 - step, 0), second + pltpu.roll(second, step, 0))
            for first, second in zip(blocks[:step], blocks[step:])
        ]
    return blocks[0]


def spread_kernel(got_ref, table_ref, out_ref, list_ref, zy_ref, x_ref, acc_ref):
    first_lane = lax.broadcasted_iota(jnp.int32, (LT, 128), 1) == 0
    zy_ref[ROWS : ROWS + LT, :] = jnp.full((LT, 128), -1.0, F32)
    x_ref[ROWS : ROWS + LT, :] = jnp.zeros((LT, 128), F32)
    total = jnp.int32(0)
    for src in range(N_ROW):
        cells = decode_cells(got_ref[src, LT])
        rows = slice(src * LT, (src + 1) * LT)
        zy_ref[rows, :] = (cells >> 8).astype(F32)
        x_ref[rows, :] = (cells & (NX - 1)).astype(F32)
        live_rows = jnp.sum(jnp.where(first_lane & (cells >= 0), 1.0, 0.0)).astype(jnp.int32)
        for j in range(LT):
            list_ref[total + j] = src * LT + j
        total = total + live_rows
    for n in range(GROUP):
        list_ref[total + n] = ROWS
    steps = (total + GROUP - 1) // GROUP
    list_ref[LIST - 1] = steps

    acc_ref[...] = jnp.zeros_like(acc_ref)
    zero = jnp.zeros((PACK, 128), BF)

    def some_rows(step, carry):
        x_lines, zy_lines = line_numbers(NX, BF), line_numbers(ZY, BF)
        left, right = [], []
        for n in range(GROUP):
            row = list_ref[step * GROUP + n]
            held = jnp.minimum(row, ROWS - 1)
            values = got_ref[held // LT, held % LT].astype(F32)
            cell = on_rows(zy_ref[pl.ds(row, 1), :], BF)
            masks = [cell == line for line in zy_lines]
            right.append(one_hot_x(x_ref[pl.ds(row, 1), :], x_lines))
            parts = []
            for c in range(FC):
                value = on_rows(values[c : c + 1], BF)
                parts += [jnp.where(mask, value, zero) for mask in masks]
            left.append(jnp.concatenate(parts, axis=0))
        acc_ref[...] += lax.dot_general(
            jnp.concatenate(left, axis=1),
            jnp.concatenate(right, axis=1),
            NT,
            preferred_element_type=F32,
        )
        return carry

    lax.fori_loop(0, steps, some_rows, 0)
    for field in range(2):
        rows = jnp.dot(
            acc_ref[field * HALF : (field + 1) * HALF, :].astype(BF),
            table_ref[...],
            preferred_element_type=F32,
        )
        if field == 1:
            rows = rows * INV
        for part in range(2):
            for group in range(CL * NY // 8):
                for half in range(2):
                    lanes = part * NX + half * 128
                    chunks = swap_chunks(
                        [
                            rows[(group * 8 + i) * ZL : (group * 8 + i + 1) * ZL, lanes : lanes + 128]
                            for i in range(8)
                        ]
                    )
                    place = field * LINES + group * 128
                    for j in range(8):
                        out_ref[
                            half * 8 + j, part * ZL : (part + 1) * ZL, place : place + 128
                        ] = chunks[j].astype(BF)


def spread(got, table_x):
    cells = jax.ShapeDtypeStruct((ROWS + LT, 128), F32)
    return pl.pallas_call(
        spread_kernel,
        out_shape=(
            jax.ShapeDtypeStruct((N_SLAB, 2 * ZL, 2 * LINES), BF),
            jax.ShapeDtypeStruct((LIST,), jnp.int32),
            cells,
            cells,
        ),
        in_specs=[VMEM] * 2,
        out_specs=(VMEM, SMEM, VMEM, VMEM),
        scratch_shapes=[pltpu.VMEM((2 * HALF, NX), F32)],
        compiler_params=PARAMS,
        name="spread",
    )(got, table_x)


def spectral_kernel(cols_ref, table_ref, filter_ref, out_ref, grad_ref, mode_ref):
    table = table_ref[...]
    cols = cols_ref[...].reshape(2 * NZ, 2 * LINES)
    mode_ref[...] = lax.dot_general(cols, table, TN, preferred_element_type=F32).astype(BF)
    filtered, cot_spec = [], []
    for c in range(CL):
        filt = filter_ref[c * KX : (c + 1) * KX, :].astype(F32)
        fr, fi = filt[:, :NZ], filt[:, NZ:]
        grad_r = jnp.zeros((KX, NZ), F32)
        grad_i = jnp.zeros((KX, NZ), F32)
        for y in range(NY):
            first = (c * NY + y) * KX
            spec = mode_ref[first : first + KX, :].astype(F32)
            cot = mode_ref[LINES + first : LINES + first + KX, :].astype(F32)
            sr, si = spec[:, :NZ], spec[:, NZ:]
            gr, gi = cot[:, :NZ], cot[:, NZ:]
            filtered.append(jnp.concatenate([sr * fr - si * fi, sr * fi + si * fr], axis=1).astype(BF))
            cot_spec.append(jnp.concatenate([gr * fr + gi * fi, gi * fr - gr * fi], axis=1).astype(BF))
            grad_r = grad_r + (gr * sr + gi * si)
            grad_i = grad_i + (gi * sr - gr * si)
        grad_ref[c * KX : (c + 1) * KX, :NZ] = grad_r
        grad_ref[c * KX : (c + 1) * KX, NZ:] = grad_i
    for field, parts in enumerate((filtered, cot_spec)):
        planes = lax.dot_general(
            table, jnp.concatenate(parts, axis=0), NT, preferred_element_type=F32
        )
        out_ref[:, :, field * LINES : (field + 1) * LINES] = planes.astype(BF).reshape(
            N_SLAB, 2 * ZL, LINES
        )


def spectral(cols, table_z, filters):
    return pl.pallas_call(
        spectral_kernel,
        out_shape=(
            jax.ShapeDtypeStruct((N_SLAB, 2 * ZL, 2 * LINES), BF),
            jax.ShapeDtypeStruct((CL * KX, 2 * NZ), F32),
        ),
        in_specs=[VMEM] * 3,
        out_specs=(VMEM,) * 2,
        scratch_shapes=[pltpu.VMEM((2 * LINES, 2 * NZ), BF)],
        compiler_params=PARAMS,
        name="spectral",
    )(cols, table_z, filters)


def gather_kernel(list_ref, plane_ref, table_ref, zy_ref, x_ref, out_ref, mode_ref, field_ref):
    for field in range(2):
        for part in range(2):
            for group in range(CL * NY // 8):
                place = field * LINES + group * 128
                for half in range(2):
                    chunks = swap_chunks(
                        [
                            plane_ref[
                                half * 8 + j, part * ZL : (part + 1) * ZL, place : place + 128
                            ].astype(F32)
                            for j in range(8)
                        ]
                    )
                    lanes = part * NX + half * 128
                    for i in range(8):
                        first = field * HALF + (group * 8 + i) * ZL
                        mode_ref[first : first + ZL, lanes : lanes + 128] = chunks[i].astype(BF)
    cells = lax.dot_general(mode_ref[...], table_ref[...], NT, preferred_element_type=F32)
    field_ref[:HALF, :] = (cells[:HALF] * INV).astype(BF)
    field_ref[HALF:, :] = cells[HALF:].astype(BF)
    out_ref[...] = jnp.zeros_like(out_ref)
    zy_line = lax.broadcasted_iota(jnp.int32, (8, 128), 0).astype(F32)

    def some_rows(step, carry):
        x_lines = line_numbers(NX, BF)
        for pair in range(0, GROUP, 2):
            rows = []
            for n in (pair, pair + 1):
                row = list_ref[step * GROUP + n]
                rows.append(jnp.where(row == ROWS, 0, row))
            picks = jnp.concatenate(
                [one_hot_x(x_ref[pl.ds(row, 1), :], x_lines) for row in rows], axis=1
            )
            lines = jnp.dot(field_ref[...], picks, preferred_element_type=F32)
            for n, row in enumerate(rows):
                cell = jnp.broadcast_to(zy_ref[pl.ds(row, 1), :], (8, 128))
                masks = [cell == zy_line + first for first in range(0, ZY, 8)]
                found = []
                for c in range(FC):
                    kept = jnp.zeros((8, 128), F32)
                    for k, mask in enumerate(masks):
                        first = c * ZY + k * 8
                        kept = jnp.where(
                            mask, lines[first : first + 8, n * 128 : (n + 1) * 128], kept
                        )
                    found.append(kept)
                out_ref[row // LT, row % LT] = sum_rows(found).astype(BF)
        return carry

    lax.fori_loop(0, list_ref[LIST - 1], some_rows, 0)


def gather(rows, planes, table_x, zy_cells, x_cells):
    return pl.pallas_call(
        gather_kernel,
        out_shape=jax.ShapeDtypeStruct((N_ROW, LT, FC, 128), BF),
        in_specs=[SMEM] + [VMEM] * 4,
        out_specs=VMEM,
        scratch_shapes=[pltpu.VMEM((2 * HALF, 2 * NX), BF), pltpu.VMEM((2 * HALF, NX), BF)],
        compiler_params=PARAMS,
        name="gather",
    )(rows, planes, table_x, zy_cells, x_cells)


def on_device(atom_feats, cotangent, filter_modes, block_tiles, cell_offsets, live_counts):
    table_x, table_z = make_tables()

    def over(axis, values):
        return lax.all_to_all(values, axis, split_axis=0, concat_axis=0, tiled=True)

    got = over("row", pack(atom_feats, cotangent, block_tiles, cell_offsets, live_counts))
    cols, rows, zy_cells, x_cells = spread(got, table_x)
    planes, grad = spectral(over("slab", cols), table_z, filter_modes.reshape(CL * KX, 2 * NZ))
    found = gather(rows, over("slab", planes), table_x, zy_cells, x_cells)
    long_range, grad_feats = unpack(over("row", found))
    return (long_range, grad_feats, grad.reshape(CL, KX, 2, NZ))


def solution(mesh):
    in_specs = (
        P(None, ("slab", "row")),
        P(None, ("slab", "row")),
        P("row", "slab", None, None),
        P(("slab", "row"), None),
        P(("slab", "row")),
        P(("slab", "row")),
    )
    out_specs = (P(None, ("slab", "row")), P(None, ("slab", "row")), P("row", "slab", None, None))
    return jax.shard_map(
        on_device, mesh=mesh, in_specs=in_specs, out_specs=out_specs, check_vma=False
    )
```

time: 194 us -> 152 us (0.78)
  blocking collectives: 10.4 us -> 66.4 us
  starting transfers between devices: 51.3 us -> 13.3 us
  Pallas kernels: 55.9 us -> 23.9 us
  waiting for transfers between devices: 67.9 us -> 43.3 us
    all_to_all x1 -> x2, blocking collectives: 10.4 us -> 66.4 us  [over(): return lax.all_to_all(values, axis, split_axis=0, concat_axis=0, tiled=True)]
    all_to_all x7 -> x2, starting transfers between devices: 51.3 us -> 13.3 us  [over(): return lax.all_to_all(values, axis, split_axis=0, concat_axis=0, tiled=True)]
    pallas_call x5, Pallas kernels: 55.9 us -> 23.9 us  [the longest x1 11 us: gather(): pl.pallas_call(gather_kernel, out_shape=jax.ShapeDtypeStruct((N_ROW, LT,...]
    all_to_all x7 -> x2, waiting for transfers between devices: 67.9 us -> 43.3 us  [over(): return lax.all_to_all(values, axis, split_axis=0, concat_axis=0, tiled=True)]
    reshape x4 -> x0, local copies, waits for them, and re-layouts: 3.53 us -> none  [the longest x1 1.08 us: on_device(): atom_feats.reshape(N_ROW, CL * LT, 128)]
    unnamed x13 -> x15, local copies, waits for them, and re-layouts: 0.04 us -> 2.58 us
  transfers between devices with their start and end apart: 7 -> 2, of which waited for: 5 -> 2; matrix products, arithmetic and copies ran while one was open for 1% -> 0% of each run, Pallas kernels for 28% -> 0%
where the time goes in v2:
time: 152 us
  blocking collectives  66.4 us (44%)
  waiting for transfers between devices  43.3 us (28%)
  Pallas kernels  23.9 us (16%)
  starting transfers between devices  13.3 us (9%)
  local copies, waits for them, and re-layouts  3.32 us (2%)
    all_to_all x2, blocking collectives, over(): return lax.all_to_all(values, axis, split_axis=0, concat_axis=0, tiled=True)  66.4 us
    all_to_all x2, waiting for transfers between devices, over(): return lax.all_to_all(values, axis, split_axis=0, concat_axis=0, tiled=True)  43.3 us
    all_to_all x2, starting transfers between devices, over(): return lax.all_to_all(values, axis, split_axis=0, concat_axis=0, tiled=True)  13.3 us
    pallas_call x1, Pallas kernels, gather(): pl.pallas_call(gather_kernel, out_shape=jax.ShapeDtypeStruct((N_ROW, LT,...  11 us
    pallas_call x1, Pallas kernels, spread(): pl.pallas_call(spread_kernel, out_shape=(jax.ShapeDtypeStruct((N_SLAB, 2...  10.3 us
  transfers between devices with their start and end apart: 2, of which 2 were waited for; matrix products, arithmetic and copies ran while one was open for 0% of the time, Pallas kernels for 0%

profile of v2, /device:TPU:1, one launch (start us, length us, event | category | flops | bytes accessed | tf_op | source)
XLA Modules:
  0.0 151.6 jit_solution(17959168569831714794)
XLA Ops:
  0.6 0.0 copy-start.4
  1.3 0.0 copy-start.5
  1.3 0.0 copy-done.4
  1.3 0.6 copy-done.5
  2.0 0.0 copy-start.2
  2.0 0.9 copy-done.2
  2.9 0.0 copy-start.3
  2.9 0.9 copy-done.3
  3.9 0.7 pack.1
  4.6 0.0 copy-start
  4.6 53.0 %all_to_all.20.got_ref = bf16[32,9,8,128]{3,2,1,0:T(8,128)(2,1)S(1)} all-to-all(bf16[32,9,8,128]{3,2,1,0:T(8,128)(2,1)S(1)} %pack.1), channel_id=1, replica_groups=mesh['slab'=16,'row'=32] {'row'}, dimensions={0} | all-to-all | bytes 1179648 | tf_op jit(solution)/shard_map/all_to_all | solution.py:399
  57.6 0.0 copy-done
  57.6 10.3 %spread.1 = (bf16[16,32,512]{2,1,0:T(8,128)(2,1)}, s32[280]{0:T(512)S(1)}, f32[264,128]{1,0:T(8,128)S(1)}, f32[264,128]{1,0:T(8,128)S(1)}) custom-call(bf16[32,9,8,128]{3,2,1,0:T(8,128)(2,1)S(1)} %all_to_all.20.got_ref, bf16[256,512]{1,0:T(8,128)(2,1)S(1)} %copy-done), custom_call_target="tpu_custom_call" | custom-call | tf_op jit(solution)/shard_map/spread/pallas_call | solution.py:268
  67.9 0.0 copy-start.6
  67.9 0.0 copy-start.1
  67.9 7.4 %all-to-all-start.1 = ((bf16[16,32,512]{2,1,0:T(8,128)(2,1)}), bf16[16,32,512]{2,1,0:T(8,128)(2,1)S(1)}, u32[]{:S(2)}, u32[]{:S(2)}) async-start(bf16[16,32,512]{2,1,0:T(8,128)(2,1)} %get-tuple-element.12), calls=%async_computation.1 | async-start | bytes 1048576 | tf_op jit(solution)/shard_map/all_to_all | solution.py:399
  75.3 0.0 copy-done.6
  75.3 10.6 %all-to-all-done.1.cols_ref = bf16[16,32,512]{2,1,0:T(8,128)(2,1)S(1)} async-done(((bf16[16,32,512]{2,1,0:T(8,128)(2,1)}), bf16[16,32,512]{2,1,0:T(8,128)(2,1)S(1)}, u32[]{:S(2)}, u32[]{:S(2)}) %all-to-all-start.1) | async-done | bytes 524320 | tf_op jit(solution)/shard_map/all_to_all | solution.py:399
  85.9 0.0 copy-done.1
  85.9 1.0 spectral.1
  86.8 13.4 %all_to_all.21.plane_ref = bf16[16,32,512]{2,1,0:T(8,128)(2,1)S(1)} all-to-all(bf16[16,32,512]{2,1,0:T(8,128)(2,1)S(1)} %get-tuple-element.13), channel_id=1, replica_groups=mesh['slab'=16,'row'=32] {'slab'}, dimensions={0} | all-to-all | bytes 1048576 | tf_op jit(solution)/shard_map/all_to_all | solution.py:399
  100.2 11.0 %gather.1 = bf16[32,8,8,128]{3,2,1,0:T(8,128)(2,1)} custom-call(s32[280]{0:T(512)S(1)} %get-tuple-element.11.list_ref, bf16[16,32,512]{2,1,0:T(8,128)(2,1)S(1)} %all_to_all.21.plane_ref, bf16[256,512]{1,0:T(8,128)(2,1)S(1)} %copy-done, f32[264,128]{1,0:T(8,128)S(1)} %get-tuple-element.14.zy_ref, f32[264,128]{1,0:T(8,128)S(1)} %get-tuple-element.15.x_ref), custom_call_target="tpu_custom_call" | custom-call | tf_op jit(solution)/shard_map/gather/pallas_call | solution.py:384
  111.2 5.9 %all-to-all-start.3 = ((bf16[32,8,8,128]{3,2,1,0:T(8,128)(2,1)}), bf16[32,8,8,128]{3,2,1,0:T(8,128)(2,1)S(1)}, u32[]{:S(2)}, u32[]{:S(2)}) async-start(bf16[32,8,8,128]{3,2,1,0:T(8,128)(2,1)} %gather.1), calls=%async_computation.3 | async-start | bytes 1048576 | tf_op jit(solution)/shard_map/all_to_all | solution.py:399
  117.1 0.7 reshape.21
  117.9 32.8 %all-to-all-done.3.in_ref = bf16[32,8,8,128]{3,2,1,0:T(8,128)(2,1)S(1)} async-done(((bf16[32,8,8,128]{3,2,1,0:T(8,128)(2,1)}), bf16[32,8,8,128]{3,2,1,0:T(8,128)(2,1)S(1)}, u32[]{:S(2)}, u32[]{:S(2)}) %all-to-all-start.3) | async-done | bytes 524320 | tf_op jit(solution)/shard_map/all_to_all | solution.py:399
  150.7 1.0 unpack.1
  (1 shorter events, 0.0 us)
Async XLA Ops:
  0.6 0.7 copy-start.4
  1.3 0.7 copy-start.5
  2.0 0.9 copy-start.2
  2.9 0.9 copy-start.3
  4.6 53.0 %copy-start = (bf16[256,512]{1,0:T(8,128)(2,1)S(1)}, bf16[256,512]{1,0:T(8,128)(2,1)}, u32[]{:S(2)}) copy-start(bf16[256,512]{1,0:T(8,128)(2,1)} %constant.9.table_ref) | copy-start | bytes 786436
  67.9 7.4 %copy-start.6 = (bf16[4,16,2,256]{3,2,1,0:T(2,128)(2,1)S(1)}, bf16[4,16,2,256]{3,2,1,0:T(2,128)(2,1)}, u32[]{:S(2)}) copy-start(bf16[4,16,2,256]{3,2,1,0:T(2,128)(2,1)} %param.10) | copy-start | bytes 196612
  67.9 18.0 %copy-start.1 = (bf16[512,512]{1,0:T(8,128)(2,1)S(1)}, bf16[512,512]{1,0:T(8,128)(2,1)}, u32[]{:S(2)}) copy-start(bf16[512,512]{1,0:T(8,128)(2,1)} %constant.10.table_ref) | copy-start | bytes 1572868
  67.9 18.0 %all-to-all-start.1 = ((bf16[16,32,512]{2,1,0:T(8,128)(2,1)}), bf16[16,32,512]{2,1,0:T(8,128)(2,1)S(1)}, u32[]{:S(2)}, u32[]{:S(2)}) async-start(bf16[16,32,512]{2,1,0:T(8,128)(2,1)} %get-tuple-element.12), calls=%async_computation.1 | async-start | bytes 1048576 | tf_op jit(solution)/shard_map/all_to_all | solution.py:399
  111.2 39.4 %all-to-all-start.3 = ((bf16[32,8,8,128]{3,2,1,0:T(8,128)(2,1)}), bf16[32,8,8,128]{3,2,1,0:T(8,128)(2,1)S(1)}, u32[]{:S(2)}, u32[]{:S(2)}) async-start(bf16[32,8,8,128]{3,2,1,0:T(8,128)(2,1)} %gather.1), calls=%async_computation.3 | async-start | bytes 1048576 | tf_op jit(solution)/shard_map/all_to_all | solution.py:399

commit v3 on v2

--- a/solution.py
+++ b/solution.py
@@ -27,6 +27,7 @@
 PACK = 16
 ROWS = N_ROW * LT
 GROUP = 16
+PIECES = 4
 LIST = ROWS + GROUP + LT
 BF = jnp.bfloat16
 F32 = jnp.float32
@@ -34,6 +35,7 @@
 TN = (((0,), (0,)), ((), ()))
 VMEM = pl.BlockSpec(memory_space=pltpu.VMEM)
 SMEM = pl.BlockSpec(memory_space=pltpu.SMEM)
+HBM = pl.BlockSpec(memory_space=pltpu.HBM)
 PARAMS = pltpu.CompilerParams(vmem_limit_bytes=32 << 20)
 
 
@@ -92,7 +94,19 @@
     return jnp.where(live, high * 128 + low, -1)
 
 
-def pack_kernel(tile_ref, live_ref, feat_ref, cot_ref, offset_ref, out_ref):
+def pack_kernel(
+    tile_ref, live_ref, feat_hbm, cot_hbm, offset_ref, out_hbm, feat_ref, cot_ref, out_ref, sems
+):
+    size = C // PIECES
+    copies = []
+    for piece in range(PIECES):
+        rows = pl.ds(piece * size, size)
+        for n, (source, held) in enumerate(((feat_hbm, feat_ref), (cot_hbm, cot_ref))):
+            copies.append(
+                pltpu.make_async_copy(source.at[rows], held.at[rows], sems.at[2 * piece + n])
+            )
+    for copy in copies:
+        copy.start()
     shape = (LT, 128)
     slot = lax.broadcasted_iota(jnp.int32, shape, 0) * 128 + lax.broadcasted_iota(
         jnp.int32, shape, 1
@@ -105,26 +119,45 @@
     zy_cell = ((offset >> 3) & (NY - 1)) * ZL + (offset >> 5)
     cells = zy_cell * NX + tile * (NX // N_ROW) + (offset & 7)
     code = encode_cells(cells, slot < live_ref[0])
-    low = lax.broadcasted_iota(jnp.int32, (FC, 128), 0) < CL
-    for j in range(LT):
-        lanes = slice(j * 128, (j + 1) * 128)
-        for pair in range(N_ROW // 2):
-            rows = slice(pair * FC, (pair + 1) * FC)
-            feat = feat_ref[rows, lanes].astype(F32)
-            cot = cot_ref[rows, lanes].astype(F32)
-            out_ref[2 * pair, j] = jnp.where(low, feat, pltpu.roll(cot, CL, 0)).astype(BF)
-            out_ref[2 * pair + 1, j] = jnp.where(low, pltpu.roll(feat, CL, 0), cot).astype(BF)
     for owner in range(N_ROW):
         out_ref[owner, LT] = code
+    low = lax.broadcasted_iota(jnp.int32, (FC, 128), 0) < CL
+    sent = []
+    for piece in range(PIECES):
+        copies[2 * piece].wait()
+        copies[2 * piece + 1].wait()
+        for pair in range(piece * size // FC, (piece + 1) * size // FC):
+            rows = slice(pair * FC, (pair + 1) * FC)
+            for j in range(LT):
+                lanes = slice(j * 128, (j + 1) * 128)
+                feat = feat_ref[rows, lanes].astype(F32)
+                cot = cot_ref[rows, lanes].astype(F32)
+                out_ref[2 * pair, j] = jnp.where(low, feat, pltpu.roll(cot, CL, 0)).astype(BF)
+                out_ref[2 * pair + 1, j] = jnp.where(low, pltpu.roll(feat, CL, 0), cot).astype(BF)
+        owners = pl.ds(piece * N_ROW // PIECES, N_ROW // PIECES)
+        sent.append(
+            pltpu.make_async_copy(
+                out_ref.at[owners], out_hbm.at[owners], sems.at[2 * PIECES + piece]
+            )
+        )
+        sent[-1].start()
+    for copy in sent:
+        copy.wait()
 
 
 def pack(atom_feats, cotangent, block_tiles, cell_offsets, live_counts):
     return pl.pallas_call(
         pack_kernel,
         out_shape=jax.ShapeDtypeStruct((N_ROW, LT + 1, FC, 128), BF),
-        in_specs=[SMEM, SMEM, VMEM, VMEM, VMEM],
-        out_specs=VMEM,
-        compiler_params=PARAMS,
+        in_specs=[SMEM, SMEM, HBM, HBM, VMEM],
+        out_specs=HBM,
+        scratch_shapes=[
+            pltpu.VMEM((C, A_DEV), BF),
+            pltpu.VMEM((C, A_DEV), BF),
+            pltpu.VMEM((N_ROW, LT + 1, FC, 128), BF),
+            pltpu.SemaphoreType.DMA((3 * PIECES,)),
+        ],
+        compiler_params=pltpu.CompilerParams(vmem_limit_bytes=60 * 1024 * 1024),
         name="pack",
     )(
         block_tiles.reshape(BLOCKS),
@@ -135,16 +168,27 @@
     )
 
 
-def unpack_kernel(in_ref, feat_ref, cot_ref):
+def unpack_kernel(in_ref, feat_hbm, cot_hbm, feat_ref, cot_ref, sems):
     low = lax.broadcasted_iota(jnp.int32, (FC, 128), 0) < CL
-    for j in range(LT):
-        lanes = slice(j * 128, (j + 1) * 128)
-        for pair in range(N_ROW // 2):
+    size = C // PIECES
+    sent = []
+    for piece in range(PIECES):
+        for pair in range(piece * size // FC, (piece + 1) * size // FC):
             rows = slice(pair * FC, (pair + 1) * FC)
-            first = in_ref[2 * pair, j].astype(F32)
-            second = in_ref[2 * pair + 1, j].astype(F32)
-            feat_ref[rows, lanes] = jnp.where(low, first, pltpu.roll(second, CL, 0)).astype(BF)
-            cot_ref[rows, lanes] = jnp.where(low, pltpu.roll(first, CL, 0), second).astype(BF)
+            for j in range(LT):
+                lanes = slice(j * 128, (j + 1) * 128)
+                first = in_ref[2 * pair, j].astype(F32)
+                second = in_ref[2 * pair + 1, j].astype(F32)
+                feat_ref[rows, lanes] = jnp.where(low, first, pltpu.roll(second, CL, 0)).astype(BF)
+                cot_ref[rows, lanes] = jnp.where(low, pltpu.roll(first, CL, 0), second).astype(BF)
+        rows = pl.ds(piece * size, size)
+        for n, (held, target) in enumerate(((feat_ref, feat_hbm), (cot_ref, cot_hbm))):
+            sent.append(
+                pltpu.make_async_copy(held.at[rows], target.at[rows], sems.at[2 * piece + n])
+            )
+            sent[-1].start()
+    for copy in sent:
+        copy.wait()
 
 
 def unpack(values):
@@ -153,7 +197,12 @@
         unpack_kernel,
         out_shape=(shape, shape),
         in_specs=[VMEM],
-        out_specs=(VMEM, VMEM),
+        out_specs=(HBM, HBM),
+        scratch_shapes=[
+            pltpu.VMEM((C, A_DEV), BF),
+            pltpu.VMEM((C, A_DEV), BF),
+            pltpu.SemaphoreType.DMA((2 * PIECES,)),
+        ],
         compiler_params=PARAMS,
         name="unpack",
     )(values)
@@ -287,8 +336,8 @@
     mode_ref[...] = lax.dot_general(cols, table, TN, preferred_element_type=F32).astype(BF)
     filtered, cot_spec = [], []
     for c in range(CL):
-        filt = filter_ref[c * KX : (c + 1) * KX, :].astype(F32)
-        fr, fi = filt[:, :NZ], filt[:, NZ:]
+        filt = filter_ref[c * KX : (c + 1) * KX].astype(F32)
+        fr, fi = filt[:, 0, :], filt[:, 1, :]
         grad_r = jnp.zeros((KX, NZ), F32)
         grad_i = jnp.zeros((KX, NZ), F32)
         for y in range(NY):
@@ -301,8 +350,8 @@
             cot_spec.append(jnp.concatenate([gr * fr + gi * fi, gi * fr - gr * fi], axis=1).astype(BF))
             grad_r = grad_r + (gr * sr + gi * si)
             grad_i = grad_i + (gi * sr - gr * si)
-        grad_ref[c * KX : (c + 1) * KX, :NZ] = grad_r
-        grad_ref[c * KX : (c + 1) * KX, NZ:] = grad_i
+        grad_ref[c * KX : (c + 1) * KX, 0, :] = grad_r
+        grad_ref[c * KX : (c + 1) * KX, 1, :] = grad_i
     for field, parts in enumerate((filtered, cot_spec)):
         planes = lax.dot_general(
             table, jnp.concatenate(parts, axis=0), NT, preferred_element_type=F32
@@ -317,7 +366,7 @@
         spectral_kernel,
         out_shape=(
             jax.ShapeDtypeStruct((N_SLAB, 2 * ZL, 2 * LINES), BF),
-            jax.ShapeDtypeStruct((CL * KX, 2 * NZ), F32),
+            jax.ShapeDtypeStruct((CL * KX, 2, NZ), F32),
         ),
         in_specs=[VMEM] * 3,
         out_specs=(VMEM,) * 2,
@@ -400,7 +449,7 @@
 
     got = over("row", pack(atom_feats, cotangent, block_tiles, cell_offsets, live_counts))
     cols, rows, zy_cells, x_cells = spread(got, table_x)
-    planes, grad = spectral(over("slab", cols), table_z, filter_modes.reshape(CL * KX, 2 * NZ))
+    planes, grad = spectral(over("slab", cols), table_z, filter_modes.reshape(CL * KX, 2, NZ))
     found = gather(rows, over("slab", planes), table_x, zy_cells, x_cells)
     long_range, grad_feats = unpack(over("row", found))
     return (long_range, grad_feats, grad.reshape(CL, KX, 2, NZ))

time: 152 us -> 148 us (0.974)
  blocking collectives: 66.4 us -> 124 us
  waiting for transfers between devices: 43.3 us -> 0 us
  starting transfers between devices: 13.3 us -> 0 us
  local copies, waits for them, and re-layouts: 3.32 us -> 0.02 us
    all_to_all x2 -> x4, blocking collectives: 66.4 us -> 124 us  [over(): return lax.all_to_all(values, axis, split_axis=0, concat_axis=0, tiled=True)]
    all_to_all x2 -> x0, waiting for transfers between devices: 43.3 us -> none  [over(): return lax.all_to_all(values, axis, split_axis=0, concat_axis=0, tiled=True)]
    all_to_all x2 -> x0, starting transfers between devices: 13.3 us -> none  [over(): return lax.all_to_all(values, axis, split_axis=0, concat_axis=0, tiled=True)]
    unnamed x15 -> x6, local copies, waits for them, and re-layouts: 2.58 us -> 0.02 us
    pallas_call x1, Pallas kernels: 0.73 us -> 2.56 us  [pack(): pl.pallas_call(pack_kernel, out_shape=jax.ShapeDtypeStruct((N_ROW, LT + 1...]
    pallas_call x1, Pallas kernels: 11 us -> 9.44 us  [gather(): pl.pallas_call(gather_kernel, out_shape=jax.ShapeDtypeStruct((N_ROW, LT,...]
    pallas_call x1, Pallas kernels: 10.3 us -> 8.75 us  [spread(): pl.pallas_call(spread_kernel, out_shape=(jax.ShapeDtypeStruct((N_SLAB, 2...]
  transfers between devices with their start and end apart: 2 -> 0, of which waited for: 2 -> 0; matrix products, arithmetic and copies ran while one was open for 0% -> 0% of each run, Pallas kernels for 0% -> 0%
where the time goes in v3:
time: 148 us
  blocking collectives  124 us (84%)
  Pallas kernels  22.9 us (15%)
    all_to_all x4, blocking collectives, over(): return lax.all_to_all(values, axis, split_axis=0, concat_axis=0, tiled=True)  124 us
    pallas_call x1, Pallas kernels, gather(): pl.pallas_call(gather_kernel, out_shape=jax.ShapeDtypeStruct((N_ROW, LT,...  9.44 us
    pallas_call x1, Pallas kernels, spread(): pl.pallas_call(spread_kernel, out_shape=(jax.ShapeDtypeStruct((N_SLAB, 2...  8.75 us

profile of v3, /device:TPU:1, one launch (start us, length us, event | category | flops | bytes accessed | tf_op | source)
XLA Modules:
  0.0 147.9 jit_solution(7125660879009935655)
XLA Ops:
  1.3 2.6 %pack.1 = bf16[32,9,8,128]{3,2,1,0:T(8,128)(2,1)} custom-call(s32[32]{0:T(128)} %bitcast.6, s32[1]{0:T(128)S(6)} %copy.11.live_ref, bf16[128,1024]{1,0:T(8,128)(2,1)} %feat_hbm.1, bf16[128,1024]{1,0:T(8,128)(2,1)} %cot_hbm.1, s32[8,128]{1,0:T(8,128)} %bitcast.5), custom_call_target="tpu_custom_call" | custom-call | tf_op jit(solution)/shard_map/pack/pallas_call | solution.py:149
  3.8 0.0 copy-start
  3.9 53.2 %all_to_all.20.got_ref = bf16[32,9,8,128]{3,2,1,0:T(8,128)(2,1)S(1)} all-to-all(bf16[32,9,8,128]{3,2,1,0:T(8,128)(2,1)} %pack.1), channel_id=1, replica_groups=mesh['slab'=16,'row'=32] {'row'}, dimensions={0} | all-to-all | bytes 1179648 | tf_op jit(solution)/shard_map/all_to_all | solution.py:448
  57.0 0.0 copy-done
  57.0 8.7 %spread.1 = (bf16[16,32,512]{2,1,0:T(8,128)(2,1)S(1)}, s32[280]{0:T(512)S(1)}, f32[264,128]{1,0:T(8,128)S(1)}, f32[264,128]{1,0:T(8,128)S(1)}) custom-call(bf16[32,9,8,128]{3,2,1,0:T(8,128)(2,1)S(1)} %all_to_all.20.got_ref, bf16[256,512]{1,0:T(8,128)(2,1)S(1)} %copy-done), custom_call_target="tpu_custom_call" | custom-call | tf_op jit(solution)/shard_map/spread/pallas_call | solution.py:317
  65.8 0.0 copy-start.1
  65.8 0.0 copy-start.2
  65.8 18.6 %all_to_all.21.cols_ref = bf16[16,32,512]{2,1,0:T(8,128)(2,1)S(1)} all-to-all(bf16[16,32,512]{2,1,0:T(8,128)(2,1)S(1)} %get-tuple-element.12), channel_id=1, replica_groups=mesh['slab'=16,'row'=32] {'slab'}, dimensions={0} | all-to-all | bytes 1048576 | tf_op jit(solution)/shard_map/all_to_all | solution.py:448
  84.4 0.0 copy-done.1
  84.4 0.0 copy-done.2
  84.4 1.3 spectral.1
  85.7 13.4 %all_to_all.22.plane_ref = bf16[16,32,512]{2,1,0:T(8,128)(2,1)S(1)} all-to-all(bf16[16,32,512]{2,1,0:T(8,128)(2,1)S(1)} %get-tuple-element.13), channel_id=1, replica_groups=mesh['slab'=16,'row'=32] {'slab'}, dimensions={0} | all-to-all | bytes 1048576 | tf_op jit(solution)/shard_map/all_to_all | solution.py:448
  99.1 9.4 %gather.1 = bf16[32,8,8,128]{3,2,1,0:T(8,128)(2,1)S(1)} custom-call(s32[280]{0:T(512)S(1)} %get-tuple-element.11.list_ref, bf16[16,32,512]{2,1,0:T(8,128)(2,1)S(1)} %all_to_all.22.plane_ref, bf16[256,512]{1,0:T(8,128)(2,1)S(1)} %copy-done, f32[264,128]{1,0:T(8,128)S(1)} %get-tuple-element.14.zy_ref, f32[264,128]{1,0:T(8,128)S(1)} %get-tuple-element.15.x_ref), custom_call_target="tpu_custom_call" | custom-call | tf_op jit(solution)/shard_map/gather/pallas_call | solution.py:433
  108.5 38.5 %all_to_all.23.in_ref = bf16[32,8,8,128]{3,2,1,0:T(8,128)(2,1)S(1)} all-to-all(bf16[32,8,8,128]{3,2,1,0:T(8,128)(2,1)S(1)} %gather.1), channel_id=1, replica_groups=mesh['slab'=16,'row'=32] {'row'}, dimensions={0} | all-to-all | bytes 1048576 | tf_op jit(solution)/shard_map/all_to_all | solution.py:448
  147.0 0.9 unpack.1
Async XLA Ops:
  3.8 53.2 %copy-start = (bf16[256,512]{1,0:T(8,128)(2,1)S(1)}, bf16[256,512]{1,0:T(8,128)(2,1)}, u32[]{:S(2)}) copy-start(bf16[256,512]{1,0:T(8,128)(2,1)} %constant.9.table_ref) | copy-start | bytes 786436
  65.8 18.6 %copy-start.1 = (bf16[512,512]{1,0:T(8,128)(2,1)S(1)}, bf16[512,512]{1,0:T(8,128)(2,1)}, u32[]{:S(2)}) copy-start(bf16[512,512]{1,0:T(8,128)(2,1)} %constant.10.table_ref) | copy-start | bytes 1572868
  65.8 18.6 %copy-start.2 = (bf16[4,16,2,256]{3,2,1,0:T(2,128)(2,1)S(1)}, bf16[4,16,2,256]{3,2,1,0:T(2,128)(2,1)}, u32[]{:S(2)}) copy-start(bf16[4,16,2,256]{3,2,1,0:T(2,128)(2,1)} %param.10) | copy-start | bytes 196612

commit v4 on v3

--- a/solution.py
+++ b/solution.py
@@ -27,6 +27,10 @@
 PACK = 16
 ROWS = N_ROW * LT
 GROUP = 16
+TILES = N_ROW
+QUARTER = 4
+PER_ROW = 128 // BLK
+TALL = 2 * FC
 PIECES = 4
 LIST = ROWS + GROUP + LT
 BF = jnp.bfloat16
@@ -52,6 +56,7 @@
     upper = np.concatenate([cos_z, -sin_z], axis=1)
     lower = np.concatenate([sin_z, cos_z], axis=1)
     table_z = np.concatenate([upper, lower], axis=0)
+    table_x = table_x.reshape(TILES, 2, QUARTER, 2 * NX).transpose(2, 0, 1, 3).reshape(NX, 2 * NX)
     table_z = table_z.reshape(2, N_SLAB, ZL, 2 * NZ).transpose(1, 0, 2, 3).reshape(2 * NZ, 2 * NZ)
     return jnp.asarray(table_x.astype(np.float32)).astype(BF), jnp.asarray(
         table_z.astype(np.float32)
@@ -208,10 +213,6 @@
     )(values)
 
 
-def on_rows(row, dtype):
-    return jnp.broadcast_to(row, (PACK, 128)).astype(dtype)
-
-
 def line_numbers(count, dtype):
     return [
         (lax.broadcasted_iota(jnp.int32, (PACK, 128), 0) + first).astype(F32).astype(dtype)
@@ -219,82 +220,123 @@
     ]
 
 
-def one_hot_x(x_row, lines):
-    cell = on_rows(x_row, BF)
+def one_hot(row, lines):
+    cell = jnp.broadcast_to(row, (PACK, 128)).astype(BF)
     one, zero = jnp.ones((PACK, 128), BF), jnp.zeros((PACK, 128), BF)
     return jnp.concatenate([jnp.where(cell == line, one, zero) for line in lines], axis=0)
 
 
-def sum_rows(blocks):
-    sub = lax.broadcasted_iota(jnp.int32, (8, 128), 0)
-    low = (sub & 4) == 0
-    blocks = [
-        jnp.where(low, first, second) + pltpu.roll(jnp.where(low, second, first), 4, 0)
-        for first, second in zip(blocks[:4], blocks[4:])
+def swap_halves(first, second):
+    low = lax.broadcasted_iota(jnp.int32, first.shape, 1) < 64
+    return (
+        jnp.where(low, first, pltpu.roll(second, 64, 1)),
+        jnp.where(low, pltpu.roll(first, 64, 1), second),
+    )
+
+
+def tile_rows(info_ref, row):
+    info = info_ref[row & (LT - 1), row >> 3]
+    return [
+        pl.multiple_of((info >> (5 * k)) & ((TILES - 1) * TALL), TALL) for k in range(PER_ROW)
     ]
-    for step in (2, 1):
-        low = (sub & step) == 0
-        blocks = [
-            jnp.where(low, first + pltpu.roll(first, 8 - step, 0), second + pltpu.roll(second, step, 0))
-            for first, second in zip(blocks[:step], blocks[step:])
-        ]
-    return blocks[0]
-
-
-def spread_kernel(got_ref, table_ref, out_ref, list_ref, zy_ref, x_ref, acc_ref):
-    first_lane = lax.broadcasted_iota(jnp.int32, (LT, 128), 1) == 0
-    zy_ref[ROWS : ROWS + LT, :] = jnp.full((LT, 128), -1.0, F32)
-    x_ref[ROWS : ROWS + LT, :] = jnp.zeros((LT, 128), F32)
+
+
+def spread_kernel(
+    got_ref, table_ref, out_ref, list_ref, info_ref, cell_ref, half_ref, held_ref, sem, mesh_ref, *accs
+):
+    lane = lax.broadcasted_iota(jnp.int32, (LT, 128), 1)
+    cell_ref[ROWS : ROWS + LT, :] = jnp.full((LT, 128), -1.0, F32)
+    half_ref[ROWS : ROWS + LT, :] = jnp.zeros((LT, 128), F32)
+    infos = jnp.zeros((LT, 128), F32)
+    for src in range(N_ROW):
+        cells = decode_cells(got_ref[src, LT])
+        live = cells >= 0
+        rows = slice(src * LT, (src + 1) * LT)
+        x_cell = cells & (NX - 1)
+        cell_ref[rows, :] = jnp.where(
+            live, (x_cell & (QUARTER - 1)) * ZY + (cells >> 8), -1
+        ).astype(F32)
+        half_ref[rows, :] = ((x_cell >> 2) & 1).astype(F32)
+        tile = ((x_cell >> 3) * TALL) << (5 * (lane // BLK))
+        tiles = jnp.sum(
+            jnp.where(live & (lane % BLK == 0), tile, 0).astype(F32), axis=1, keepdims=True
+        )
+        count = jnp.sum(jnp.where(live & (lane == 0), 1.0, 0.0), keepdims=True)
+        infos = jnp.where(lane == src, jnp.broadcast_to(tiles, (LT, 128)), infos)
+        infos = jnp.where(lane == 64 + src, jnp.broadcast_to(count, (LT, 128)), infos)
+    held_ref[...] = infos.astype(jnp.int32)
+    copy = pltpu.make_async_copy(held_ref, info_ref, sem)
+    copy.start()
+    for acc in accs:
+        acc[...] = jnp.zeros_like(acc)
+    copy.wait()
     total = jnp.int32(0)
     for src in range(N_ROW):
-        cells = decode_cells(got_ref[src, LT])
-        rows = slice(src * LT, (src + 1) * LT)
-        zy_ref[rows, :] = (cells >> 8).astype(F32)
-        x_ref[rows, :] = (cells & (NX - 1)).astype(F32)
-        live_rows = jnp.sum(jnp.where(first_lane & (cells >= 0), 1.0, 0.0)).astype(jnp.int32)
         for j in range(LT):
             list_ref[total + j] = src * LT + j
-        total = total + live_rows
+        total = total + info_ref[0, 64 + src]
     for n in range(GROUP):
         list_ref[total + n] = ROWS
     steps = (total + GROUP - 1) // GROUP
     list_ref[LIST - 1] = steps
 
-    acc_ref[...] = jnp.zeros_like(acc_ref)
-    zero = jnp.zeros((PACK, 128), BF)
+    zero = jnp.zeros((TALL, 128), BF)
+    upper = (lax.broadcasted_iota(jnp.int32, (TALL, 128), 0) // FC).astype(F32).astype(BF)
+    block = (lax.broadcasted_iota(jnp.int32, (TALL, 128), 1) // BLK).astype(F32).astype(BF)
 
     def some_rows(step, carry):
-        x_lines, zy_lines = line_numbers(NX, BF), line_numbers(ZY, BF)
-        left, right = [], []
-        for n in range(GROUP):
-            row = list_ref[step * GROUP + n]
-            held = jnp.minimum(row, ROWS - 1)
-            values = got_ref[held // LT, held % LT].astype(F32)
-            cell = on_rows(zy_ref[pl.ds(row, 1), :], BF)
-            masks = [cell == line for line in zy_lines]
-            right.append(one_hot_x(x_ref[pl.ds(row, 1), :], x_lines))
-            parts = []
-            for c in range(FC):
-                value = on_rows(values[c : c + 1], BF)
-                parts += [jnp.where(mask, value, zero) for mask in masks]
-            left.append(jnp.concatenate(parts, axis=0))
-        acc_ref[...] += lax.dot_general(
-            jnp.concatenate(left, axis=1),
-            jnp.concatenate(right, axis=1),
-            NT,
+        lines = line_numbers(NX, BF)
+        for pair in range(0, GROUP, 2):
+            right, left, places = [], [], []
+            for n in range(2):
+                row = list_ref[step * GROUP + pair + n]
+                held = jnp.minimum(row, ROWS - 1)
+                values = got_ref[held >> 3, held & (LT - 1)].astype(F32)
+                half = jnp.broadcast_to(half_ref[pl.ds(row, 1), :], (TALL, 128)).astype(BF)
+                values = jnp.where(
+                    half == upper, jnp.concatenate([values, values], axis=0).astype(BF), zero
+                )
+                right.append(one_hot(cell_ref[pl.ds(row, 1), :], lines))
+                mine = [jnp.where(block == float(k), values, zero) for k in range(PER_ROW)]
+                none = [zero] * PER_ROW
+                left.append(jnp.concatenate(mine + none if n == 0 else none + mine, axis=0))
+                places += tile_rows(info_ref, row)
+            sums = lax.dot_general(
+                jnp.concatenate(left, axis=1),
+                jnp.concatenate(right, axis=1),
+                NT,
+                preferred_element_type=F32,
+            )
+            for k, place in enumerate(places):
+                for col in range(2):
+                    acc = accs[2 * (k % PER_ROW) + col]
+                    acc[pl.ds(place, TALL), :] += sums[
+                        k * TALL : (k + 1) * TALL, col * 128 : (col + 1) * 128
+                    ]
+        return carry
+
+    lax.fori_loop(0, steps, some_rows, 0)
+    for col in range(2):
+        accs[col][...] += accs[2 + col][...] + accs[4 + col][...] + accs[6 + col][...]
+    for pair in range(FC // 2):
+        for col in range(2):
+            even, odd = (
+                accs[col][pl.ds(2 * pair + n, 2 * TILES, stride=FC), :]
+                for n in range(2)
+            )
+            for n, block_rows in enumerate(swap_halves(even, odd)):
+                first = (2 * col + n) * 2 * TILES
+                mesh_ref[first : first + 2 * TILES, pair * 128 : (pair + 1) * 128] = (
+                    block_rows.astype(BF)
+                )
+    for field in range(2):
+        rows = lax.dot_general(
+            mesh_ref[:, field * HALF : (field + 1) * HALF],
+            table_ref[...],
+            TN,
             preferred_element_type=F32,
         )
-        return carry
-
-    lax.fori_loop(0, steps, some_rows, 0)
-    for field in range(2):
-        rows = jnp.dot(
-            acc_ref[field * HALF : (field + 1) * HALF, :].astype(BF),
-            table_ref[...],
-            preferred_element_type=F32,
-        )
-        if field == 1:
-            rows = rows * INV
+        rows = (rows * INV if field == 1 else rows).astype(BF)
         for part in range(2):
             for group in range(CL * NY // 8):
                 for half in range(2):
@@ -309,7 +351,7 @@
                     for j in range(8):
                         out_ref[
                             half * 8 + j, part * ZL : (part + 1) * ZL, place : place + 128
-                        ] = chunks[j].astype(BF)
+                        ] = chunks[j]
 
 
 def spread(got, table_x):
@@ -319,12 +361,18 @@
         out_shape=(
             jax.ShapeDtypeStruct((N_SLAB, 2 * ZL, 2 * LINES), BF),
             jax.ShapeDtypeStruct((LIST,), jnp.int32),
+            jax.ShapeDtypeStruct((LT, 128), jnp.int32),
             cells,
             cells,
         ),
         in_specs=[VMEM] * 2,
-        out_specs=(VMEM, SMEM, VMEM, VMEM),
-        scratch_shapes=[pltpu.VMEM((2 * HALF, NX), F32)],
+        out_specs=(VMEM, SMEM, SMEM, VMEM, VMEM),
+        scratch_shapes=[
+            pltpu.VMEM((LT, 128), jnp.int32),
+            pltpu.SemaphoreType.DMA(()),
+            pltpu.VMEM((NX, 2 * HALF), BF),
+        ]
+        + [pltpu.VMEM((TILES * TALL, 128), F32)] * (2 * PER_ROW),
         compiler_params=PARAMS,
         name="spread",
     )(got, table_x)
@@ -376,7 +424,9 @@
     )(cols, table_z, filters)
 
 
-def gather_kernel(list_ref, plane_ref, table_ref, zy_ref, x_ref, out_ref, mode_ref, field_ref):
+def gather_kernel(
+    list_ref, info_ref, plane_ref, table_ref, cell_ref, half_ref, out_ref, mode_ref, field_ref, *wide_refs
+):
     for field in range(2):
         for part in range(2):
             for group in range(CL * NY // 8):
@@ -386,59 +436,86 @@
                         [
                             plane_ref[
                                 half * 8 + j, part * ZL : (part + 1) * ZL, place : place + 128
-                            ].astype(F32)
+                            ]
                             for j in range(8)
                         ]
                     )
                     lanes = part * NX + half * 128
                     for i in range(8):
                         first = field * HALF + (group * 8 + i) * ZL
-                        mode_ref[first : first + ZL, lanes : lanes + 128] = chunks[i].astype(BF)
-    cells = lax.dot_general(mode_ref[...], table_ref[...], NT, preferred_element_type=F32)
-    field_ref[:HALF, :] = (cells[:HALF] * INV).astype(BF)
-    field_ref[HALF:, :] = cells[HALF:].astype(BF)
+                        mode_ref[first : first + ZL, lanes : lanes + 128] = chunks[i]
+    for field in range(2):
+        cells = lax.dot_general(
+            table_ref[...],
+            mode_ref[field * HALF : (field + 1) * HALF, :],
+            NT,
+            preferred_element_type=F32,
+        )
+        if field == 0:
+            cells = cells * INV
+        for pair in range(CL // 2):
+            lanes = slice(pair * 128, (pair + 1) * 128)
+            for col in range(2):
+                first = 2 * col * 2 * TILES
+                swapped = swap_halves(
+                    cells[first : first + 2 * TILES, lanes],
+                    cells[first + 2 * TILES : first + 4 * TILES, lanes],
+                )
+                for n in range(2):
+                    wide_refs[col][
+                        pl.ds(field * CL + 2 * pair + n, 2 * TILES, stride=FC), :
+                    ] = swapped[n]
+    for col in range(2):
+        field_ref[:, col * 128 : (col + 1) * 128] = wide_refs[col][...].astype(BF)
     out_ref[...] = jnp.zeros_like(out_ref)
-    zy_line = lax.broadcasted_iota(jnp.int32, (8, 128), 0).astype(F32)
+    block = 2.0 * (lax.broadcasted_iota(jnp.int32, (FC, 128), 1) // BLK).astype(F32)
 
     def some_rows(step, carry):
-        x_lines = line_numbers(NX, BF)
+        lines = line_numbers(NX, BF)
         for pair in range(0, GROUP, 2):
-            rows = []
-            for n in (pair, pair + 1):
-                row = list_ref[step * GROUP + n]
-                rows.append(jnp.where(row == ROWS, 0, row))
-            picks = jnp.concatenate(
-                [one_hot_x(x_ref[pl.ds(row, 1), :], x_lines) for row in rows], axis=1
+            rows, places, picks = [], [], []
+            for n in range(2):
+                row = list_ref[step * GROUP + pair + n]
+                row = jnp.where(row == ROWS, 0, row)
+                rows.append(row)
+                places += tile_rows(info_ref, row)
+                picks.append(one_hot(cell_ref[pl.ds(row, 1), :], lines))
+            found = jnp.dot(
+                jnp.concatenate([field_ref[pl.ds(place, TALL), :] for place in places], axis=0),
+                jnp.concatenate(picks, axis=1),
+                preferred_element_type=F32,
             )
-            lines = jnp.dot(field_ref[...], picks, preferred_element_type=F32)
             for n, row in enumerate(rows):
-                cell = jnp.broadcast_to(zy_ref[pl.ds(row, 1), :], (8, 128))
-                masks = [cell == zy_line + first for first in range(0, ZY, 8)]
-                found = []
-                for c in range(FC):
-                    kept = jnp.zeros((8, 128), F32)
-                    for k, mask in enumerate(masks):
-                        first = c * ZY + k * 8
-                        kept = jnp.where(
-                            mask, lines[first : first + 8, n * 128 : (n + 1) * 128], kept
-                        )
-                    found.append(kept)
-                out_ref[row // LT, row % LT] = sum_rows(found).astype(BF)
+                wanted = block + jnp.broadcast_to(half_ref[pl.ds(row, 1), :], (FC, 128))
+                kept = jnp.zeros((FC, 128), F32)
+                for k in range(2 * PER_ROW):
+                    first = n * PER_ROW * TALL + k * FC
+                    kept = jnp.where(
+                        wanted == float(k),
+                        found[first : first + FC, n * 128 : (n + 1) * 128],
+                        kept,
+                    )
+                out_ref[row >> 3, row & (LT - 1)] = kept.astype(BF)
         return carry
 
     lax.fori_loop(0, list_ref[LIST - 1], some_rows, 0)
 
 
-def gather(rows, planes, table_x, zy_cells, x_cells):
+def gather(rows, infos, planes, table_x, cells, halves):
     return pl.pallas_call(
         gather_kernel,
         out_shape=jax.ShapeDtypeStruct((N_ROW, LT, FC, 128), BF),
-        in_specs=[SMEM] + [VMEM] * 4,
+        in_specs=[SMEM] * 2 + [VMEM] * 4,
         out_specs=VMEM,
-        scratch_shapes=[pltpu.VMEM((2 * HALF, 2 * NX), BF), pltpu.VMEM((2 * HALF, NX), BF)],
+        scratch_shapes=[
+            pltpu.VMEM((2 * HALF, 2 * NX), BF),
+            pltpu.VMEM((TILES * TALL, NX), BF),
+            pltpu.VMEM((TILES * TALL, 128), F32),
+            pltpu.VMEM((TILES * TALL, 128), F32),
+        ],
         compiler_params=PARAMS,
         name="gather",
-    )(rows, planes, table_x, zy_cells, x_cells)
+    )(rows, infos, planes, table_x, cells, halves)
 
 
 def on_device(atom_feats, cotangent, filter_modes, block_tiles, cell_offsets, live_counts):
@@ -448,9 +525,9 @@
         return lax.all_to_all(values, axis, split_axis=0, concat_axis=0, tiled=True)
 
     got = over("row", pack(atom_feats, cotangent, block_tiles, cell_offsets, live_counts))
-    cols, rows, zy_cells, x_cells = spread(got, table_x)
+    cols, rows, infos, cells, halves = spread(got, table_x)
     planes, grad = spectral(over("slab", cols), table_z, filter_modes.reshape(CL * KX, 2, NZ))
-    found = gather(rows, over("slab", planes), table_x, zy_cells, x_cells)
+    found = gather(rows, infos, over("slab", planes), table_x, cells, halves)
     long_range, grad_feats = unpack(over("row", found))
     return (long_range, grad_feats, grad.reshape(CL, KX, 2, NZ))
 

time: 148 us -> 142 us (0.959)
  Pallas kernels: 22.9 us -> 16.9 us
    pallas_call x1, Pallas kernels: 9.44 us -> 4.86 us  [gather(): pl.pallas_call(gather_kernel, out_shape=jax.ShapeDtypeStruct((N_ROW, LT,...]
where the time goes in v4:
time: 142 us; the launch traced here: 141 us
  blocking collectives  123 us (87%)
  Pallas kernels  16.9 us (12%)
    all_to_all x4, blocking collectives, over(): return lax.all_to_all(values, axis, split_axis=0, concat_axis=0, tiled=True)  123 us
    pallas_call x1, Pallas kernels, spread(): pl.pallas_call(spread_kernel, out_shape=(jax.ShapeDtypeStruct((N_SLAB, 2...  7.33 us
    pallas_call x1, Pallas kernels, gather(): pl.pallas_call(gather_kernel, out_shape=jax.ShapeDtypeStruct((N_ROW, LT,...  4.86 us

profile of v4, /device:TPU:1, one launch (start us, length us, event | category | flops | bytes accessed | tf_op | source)
XLA Modules:
  0.0 141.4 jit_solution(5667386323405059807)
XLA Ops:
  1.3 2.6 %pack.1 = bf16[32,9,8,128]{3,2,1,0:T(8,128)(2,1)} custom-call(s32[32]{0:T(128)} %bitcast.6, s32[1]{0:T(128)S(6)} %copy.11.live_ref, bf16[128,1024]{1,0:T(8,128)(2,1)} %feat_hbm.1, bf16[128,1024]{1,0:T(8,128)(2,1)} %cot_hbm.1, s32[8,128]{1,0:T(8,128)} %bitcast.5), custom_call_target="tpu_custom_call" | custom-call | tf_op jit(solution)/shard_map/pack/pallas_call | solution.py:154
  3.8 0.0 copy-start
  3.9 53.2 %all_to_all.20.got_ref = bf16[32,9,8,128]{3,2,1,0:T(8,128)(2,1)S(1)} all-to-all(bf16[32,9,8,128]{3,2,1,0:T(8,128)(2,1)} %pack.1), channel_id=1, replica_groups=mesh['slab'=16,'row'=32] {'row'}, dimensions={0} | all-to-all | bytes 1179648 | tf_op jit(solution)/shard_map/all_to_all | solution.py:525
  57.0 0.0 copy-done
  57.0 7.3 %spread.1 = (bf16[16,32,512]{2,1,0:T(8,128)(2,1)S(1)}, s32[280]{0:T(512)S(1)}, s32[8,128]{1,0:T(8,128)S(1)}, f32[264,128]{1,0:T(8,128)S(1)}, f32[264,128]{1,0:T(8,128)S(1)}) custom-call(bf16[32,9,8,128]{3,2,1,0:T(8,128)(2,1)S(1)} %all_to_all.20.got_ref, bf16[256,512]{1,0:T(8,128)(2,1)S(1)} %copy-done), custom_call_target="tpu_custom_call" | custom-call | tf_op jit(solution)/shard_map/spread/pallas_call | solution.py:359
  64.4 0.0 copy-start.1
  64.4 0.0 copy-start.2
  64.4 18.1 %all_to_all.21.cols_ref = bf16[16,32,512]{2,1,0:T(8,128)(2,1)S(1)} all-to-all(bf16[16,32,512]{2,1,0:T(8,128)(2,1)S(1)} %get-tuple-element.14), channel_id=1, replica_groups=mesh['slab'=16,'row'=32] {'slab'}, dimensions={0} | all-to-all | bytes 1048576 | tf_op jit(solution)/shard_map/all_to_all | solution.py:525
  82.5 0.0 copy-done.1
  82.5 0.0 copy-done.2
  82.5 1.3 spectral.1
  83.8 13.4 %all_to_all.22.plane_ref = bf16[16,32,512]{2,1,0:T(8,128)(2,1)S(1)} all-to-all(bf16[16,32,512]{2,1,0:T(8,128)(2,1)S(1)} %get-tuple-element.15), channel_id=1, replica_groups=mesh['slab'=16,'row'=32] {'slab'}, dimensions={0} | all-to-all | bytes 1048576 | tf_op jit(solution)/shard_map/all_to_all | solution.py:525
  97.2 4.9 %gather.1 = bf16[32,8,8,128]{3,2,1,0:T(8,128)(2,1)S(1)} custom-call(s32[280]{0:T(512)S(1)} %get-tuple-element.12.list_ref, s32[8,128]{1,0:T(8,128)S(1)} %get-tuple-element.13.info_ref, bf16[16,32,512]{2,1,0:T(8,128)(2,1)S(1)} %all_to_all.22.plane_ref, bf16[256,512]{1,0:T(8,128)(2,1)S(1)} %copy-done, f32[264,128]{1,0:T(8,128)S(1)} %get-tuple-element.16.cell_ref, ...), custom_call_target="tpu_custom_call" | custom-call | tf_op jit(solution)/shard_map/gather/pallas_call | solution.py:505
  102.0 38.5 %all_to_all.23.in_ref = bf16[32,8,8,128]{3,2,1,0:T(8,128)(2,1)S(1)} all-to-all(bf16[32,8,8,128]{3,2,1,0:T(8,128)(2,1)S(1)} %gather.1), channel_id=1, replica_groups=mesh['slab'=16,'row'=32] {'row'}, dimensions={0} | all-to-all | bytes 1048576 | tf_op jit(solution)/shard_map/all_to_all | solution.py:525
  140.6 0.9 unpack.1
Async XLA Ops:
  3.8 53.2 %copy-start = (bf16[256,512]{1,0:T(8,128)(2,1)S(1)}, bf16[256,512]{1,0:T(8,128)(2,1)}, u32[]{:S(2)}) copy-start(bf16[256,512]{1,0:T(8,128)(2,1)} %constant.9.table_ref) | copy-start | bytes 786436
  64.4 18.1 %copy-start.1 = (bf16[512,512]{1,0:T(8,128)(2,1)S(1)}, bf16[512,512]{1,0:T(8,128)(2,1)}, u32[]{:S(2)}) copy-start(bf16[512,512]{1,0:T(8,128)(2,1)} %constant.10.table_ref) | copy-start | bytes 1572868
  64.4 18.1 %copy-start.2 = (bf16[4,16,2,256]{3,2,1,0:T(2,128)(2,1)S(1)}, bf16[4,16,2,256]{3,2,1,0:T(2,128)(2,1)}, u32[]{:S(2)}) copy-start(bf16[4,16,2,256]{3,2,1,0:T(2,128)(2,1)} %param.10) | copy-start | bytes 196612

commit v5 on v4

--- a/solution.py
+++ b/solution.py
@@ -26,11 +26,12 @@
 INV = 1.0 / (NX * NZ)
 PACK = 16
 ROWS = N_ROW * LT
-GROUP = 16
+GROUP = 32
 TILES = N_ROW
 QUARTER = 4
 PER_ROW = 128 // BLK
 TALL = 2 * FC
+SETS = 2
 PIECES = 4
 LIST = ROWS + GROUP + LT
 BF = jnp.bfloat16
@@ -100,9 +101,16 @@
 
 
 def pack_kernel(
-    tile_ref, live_ref, feat_hbm, cot_hbm, offset_ref, out_hbm, feat_ref, cot_ref, out_ref, sems
+    tile_hbm, live_hbm, feat_hbm, cot_hbm, offset_hbm, out_hbm,
+    tile_ref, live_ref, feat_ref, cot_ref, offset_ref, out_ref, sems,
 ):
     size = C // PIECES
+    small = [
+        pltpu.make_async_copy(source, held, sems.at[3 * PIECES + n])
+        for n, (source, held) in enumerate(
+            ((tile_hbm, tile_ref), (live_hbm, live_ref), (offset_hbm, offset_ref))
+        )
+    ]
     copies = []
     for piece in range(PIECES):
         rows = pl.ds(piece * size, size)
@@ -110,8 +118,10 @@
             copies.append(
                 pltpu.make_async_copy(source.at[rows], held.at[rows], sems.at[2 * piece + n])
             )
-    for copy in copies:
+    for copy in small + copies:
         copy.start()
+    for copy in small:
+        copy.wait()
     shape = (LT, 128)
     slot = lax.broadcasted_iota(jnp.int32, shape, 0) * 128 + lax.broadcasted_iota(
         jnp.int32, shape, 1
@@ -123,7 +133,7 @@
     offset = offset_ref[...]
     zy_cell = ((offset >> 3) & (NY - 1)) * ZL + (offset >> 5)
     cells = zy_cell * NX + tile * (NX // N_ROW) + (offset & 7)
-    code = encode_cells(cells, slot < live_ref[0])
+    code = encode_cells(cells, slot < live_ref[0, 0])
     for owner in range(N_ROW):
         out_ref[owner, LT] = code
     low = lax.broadcasted_iota(jnp.int32, (FC, 128), 0) < CL
@@ -154,19 +164,22 @@
     return pl.pallas_call(
         pack_kernel,
         out_shape=jax.ShapeDtypeStruct((N_ROW, LT + 1, FC, 128), BF),
-        in_specs=[SMEM, SMEM, HBM, HBM, VMEM],
+        in_specs=[HBM] * 5,
         out_specs=HBM,
         scratch_shapes=[
+            pltpu.SMEM((BLOCKS,), jnp.int32),
+            pltpu.SMEM((1, 1), jnp.int32),
             pltpu.VMEM((C, A_DEV), BF),
             pltpu.VMEM((C, A_DEV), BF),
+            pltpu.VMEM((LT, 128), jnp.int32),
             pltpu.VMEM((N_ROW, LT + 1, FC, 128), BF),
-            pltpu.SemaphoreType.DMA((3 * PIECES,)),
+            pltpu.SemaphoreType.DMA((3 * PIECES + 3,)),
         ],
         compiler_params=pltpu.CompilerParams(vmem_limit_bytes=60 * 1024 * 1024),
         name="pack",
     )(
         block_tiles.reshape(BLOCKS),
-        live_counts,
+        live_counts.reshape(1, 1),
         atom_feats,
         cotangent,
         cell_offsets.reshape(LT, 128),
@@ -248,6 +261,7 @@
     cell_ref[ROWS : ROWS + LT, :] = jnp.full((LT, 128), -1.0, F32)
     half_ref[ROWS : ROWS + LT, :] = jnp.zeros((LT, 128), F32)
     infos = jnp.zeros((LT, 128), F32)
+    total = jnp.int32(0)
     for src in range(N_ROW):
         cells = decode_cells(got_ref[src, LT])
         live = cells >= 0
@@ -261,20 +275,16 @@
         tiles = jnp.sum(
             jnp.where(live & (lane % BLK == 0), tile, 0).astype(F32), axis=1, keepdims=True
         )
-        count = jnp.sum(jnp.where(live & (lane == 0), 1.0, 0.0), keepdims=True)
+        for j in range(LT):
+            list_ref[total + j] = src * LT + j
+        total = total + jnp.sum(jnp.where(live & (lane == 0), 1.0, 0.0)).astype(jnp.int32)
         infos = jnp.where(lane == src, jnp.broadcast_to(tiles, (LT, 128)), infos)
-        infos = jnp.where(lane == 64 + src, jnp.broadcast_to(count, (LT, 128)), infos)
     held_ref[...] = infos.astype(jnp.int32)
     copy = pltpu.make_async_copy(held_ref, info_ref, sem)
     copy.start()
     for acc in accs:
         acc[...] = jnp.zeros_like(acc)
     copy.wait()
-    total = jnp.int32(0)
-    for src in range(N_ROW):
-        for j in range(LT):
-            list_ref[total + j] = src * LT + j
-        total = total + info_ref[0, 64 + src]
     for n in range(GROUP):
         list_ref[total + n] = ROWS
     steps = (total + GROUP - 1) // GROUP
@@ -309,7 +319,7 @@
             )
             for k, place in enumerate(places):
                 for col in range(2):
-                    acc = accs[2 * (k % PER_ROW) + col]
+                    acc = accs[2 * (k % SETS) + col]
                     acc[pl.ds(place, TALL), :] += sums[
                         k * TALL : (k + 1) * TALL, col * 128 : (col + 1) * 128
                     ]
@@ -317,7 +327,7 @@
 
     lax.fori_loop(0, steps, some_rows, 0)
     for col in range(2):
-        accs[col][...] += accs[2 + col][...] + accs[4 + col][...] + accs[6 + col][...]
+        accs[col][...] += accs[2 + col][...]
     for pair in range(FC // 2):
         for col in range(2):
             even, odd = (
@@ -372,7 +382,7 @@
             pltpu.SemaphoreType.DMA(()),
             pltpu.VMEM((NX, 2 * HALF), BF),
         ]
-        + [pltpu.VMEM((TILES * TALL, 128), F32)] * (2 * PER_ROW),
+        + [pltpu.VMEM((TILES * TALL, 128), F32)] * (2 * SETS),
         compiler_params=PARAMS,
         name="spread",
     )(got, table_x)

time: 142 us -> 140 us (0.986)
  Pallas kernels: 16.9 us -> 14.7 us
where the time goes in v5:
time: 140 us; the launch traced here: 139 us
  blocking collectives  123 us (88%)
  Pallas kernels  14.7 us (10%)
    all_to_all x4, blocking collectives, over(): return lax.all_to_all(values, axis, split_axis=0, concat_axis=0, tiled=True)  123 us
    pallas_call x1, Pallas kernels, spread(): pl.pallas_call(spread_kernel, out_shape=(jax.ShapeDtypeStruct((N_SLAB, 2...  6.5 us
    pallas_call x1, Pallas kernels, gather(): pl.pallas_call(gather_kernel, out_shape=jax.ShapeDtypeStruct((N_ROW, LT,...  4.17 us

profile of v5, /device:TPU:1, one launch (start us, length us, event | category | flops | bytes accessed | tf_op | source)
XLA Modules:
  0.0 139.3 jit_solution(5137406401598546781)
XLA Ops:
  1.3 1.9 %pack.1 = bf16[32,9,8,128]{3,2,1,0:T(8,128)(2,1)} custom-call(s32[32]{0:T(128)} %bitcast.8, s32[1,1]{1,0:T(1,128)} %bitcast.5.live_hbm, bf16[128,1024]{1,0:T(8,128)(2,1)} %feat_hbm.1, bf16[128,1024]{1,0:T(8,128)(2,1)} %cot_hbm.1, s32[8,128]{1,0:T(8,128)} %bitcast.7), custom_call_target="tpu_custom_call" | custom-call | tf_op jit(solution)/shard_map/pack/pallas_call | solution.py:164
  3.2 0.0 copy-start
  3.2 53.2 %all_to_all.20.got_ref = bf16[32,9,8,128]{3,2,1,0:T(8,128)(2,1)S(1)} all-to-all(bf16[32,9,8,128]{3,2,1,0:T(8,128)(2,1)} %pack.1), channel_id=1, replica_groups=mesh['slab'=16,'row'=32] {'row'}, dimensions={0} | all-to-all | bytes 1179648 | tf_op jit(solution)/shard_map/all_to_all | solution.py:535
  56.4 0.0 copy-done
  56.4 6.5 %spread.1 = (bf16[16,32,512]{2,1,0:T(8,128)(2,1)S(1)}, s32[296]{0:T(512)S(1)}, s32[8,128]{1,0:T(8,128)S(1)}, f32[264,128]{1,0:T(8,128)S(1)}, f32[264,128]{1,0:T(8,128)S(1)}) custom-call(bf16[32,9,8,128]{3,2,1,0:T(8,128)(2,1)S(1)} %all_to_all.20.got_ref, bf16[256,512]{1,0:T(8,128)(2,1)S(1)} %copy-done), custom_call_target="tpu_custom_call" | custom-call | tf_op jit(solution)/shard_map/spread/pallas_call | solution.py:369
  62.9 0.0 copy-start.1
  62.9 0.0 copy-start.2
  62.9 18.2 %all_to_all.21.cols_ref = bf16[16,32,512]{2,1,0:T(8,128)(2,1)S(1)} all-to-all(bf16[16,32,512]{2,1,0:T(8,128)(2,1)S(1)} %get-tuple-element.14), channel_id=1, replica_groups=mesh['slab'=16,'row'=32] {'slab'}, dimensions={0} | all-to-all | bytes 1048576 | tf_op jit(solution)/shard_map/all_to_all | solution.py:535
  81.1 0.0 copy-done.1
  81.1 0.0 copy-done.2
  81.1 1.3 spectral.1
  82.4 13.4 %all_to_all.22.plane_ref = bf16[16,32,512]{2,1,0:T(8,128)(2,1)S(1)} all-to-all(bf16[16,32,512]{2,1,0:T(8,128)(2,1)S(1)} %get-tuple-element.15), channel_id=1, replica_groups=mesh['slab'=16,'row'=32] {'slab'}, dimensions={0} | all-to-all | bytes 1048576 | tf_op jit(solution)/shard_map/all_to_all | solution.py:535
  95.8 4.2 %gather.1 = bf16[32,8,8,128]{3,2,1,0:T(8,128)(2,1)S(1)} custom-call(s32[296]{0:T(512)S(1)} %get-tuple-element.12.list_ref, s32[8,128]{1,0:T(8,128)S(1)} %get-tuple-element.13.info_ref, bf16[16,32,512]{2,1,0:T(8,128)(2,1)S(1)} %all_to_all.22.plane_ref, bf16[256,512]{1,0:T(8,128)(2,1)S(1)} %copy-done, f32[264,128]{1,0:T(8,128)S(1)} %get-tuple-element.16.cell_ref, ...), custom_call_target="tpu_custom_call" | custom-call | tf_op jit(solution)/shard_map/gather/pallas_call | solution.py:515
  99.9 38.5 %all_to_all.23.in_ref = bf16[32,8,8,128]{3,2,1,0:T(8,128)(2,1)S(1)} all-to-all(bf16[32,8,8,128]{3,2,1,0:T(8,128)(2,1)S(1)} %gather.1), channel_id=1, replica_groups=mesh['slab'=16,'row'=32] {'row'}, dimensions={0} | all-to-all | bytes 1048576 | tf_op jit(solution)/shard_map/all_to_all | solution.py:535
  138.5 0.9 unpack.1
Async XLA Ops:
  3.2 53.2 %copy-start = (bf16[256,512]{1,0:T(8,128)(2,1)S(1)}, bf16[256,512]{1,0:T(8,128)(2,1)}, u32[]{:S(2)}) copy-start(bf16[256,512]{1,0:T(8,128)(2,1)} %constant.9.table_ref) | copy-start | bytes 786436
  62.9 18.2 %copy-start.1 = (bf16[512,512]{1,0:T(8,128)(2,1)S(1)}, bf16[512,512]{1,0:T(8,128)(2,1)}, u32[]{:S(2)}) copy-start(bf16[512,512]{1,0:T(8,128)(2,1)} %constant.10.table_ref) | copy-start | bytes 1572868
  62.9 18.2 %copy-start.2 = (bf16[4,16,2,256]{3,2,1,0:T(2,128)(2,1)S(1)}, bf16[4,16,2,256]{3,2,1,0:T(2,128)(2,1)}, u32[]{:S(2)}) copy-start(bf16[4,16,2,256]{3,2,1,0:T(2,128)(2,1)} %param.10) | copy-start | bytes 196612

commit v6 on v5

--- a/solution.py
+++ b/solution.py
@@ -32,7 +32,7 @@
 PER_ROW = 128 // BLK
 TALL = 2 * FC
 SETS = 2
-PIECES = 4
+PIECES = 8
 LIST = ROWS + GROUP + LT
 BF = jnp.bfloat16
 F32 = jnp.float32
@@ -331,14 +331,12 @@
     for pair in range(FC // 2):
         for col in range(2):
             even, odd = (
-                accs[col][pl.ds(2 * pair + n, 2 * TILES, stride=FC), :]
+                accs[col][pl.ds(2 * pair + n, 2 * TILES, stride=FC), :].astype(BF)
                 for n in range(2)
             )
             for n, block_rows in enumerate(swap_halves(even, odd)):
                 first = (2 * col + n) * 2 * TILES
-                mesh_ref[first : first + 2 * TILES, pair * 128 : (pair + 1) * 128] = (
-                    block_rows.astype(BF)
-                )
+                mesh_ref[first : first + 2 * TILES, pair * 128 : (pair + 1) * 128] = block_rows
     for field in range(2):
         rows = lax.dot_general(
             mesh_ref[:, field * HALF : (field + 1) * HALF],
@@ -394,8 +392,8 @@
     mode_ref[...] = lax.dot_general(cols, table, TN, preferred_element_type=F32).astype(BF)
     filtered, cot_spec = [], []
     for c in range(CL):
-        filt = filter_ref[c * KX : (c + 1) * KX].astype(F32)
-        fr, fi = filt[:, 0, :], filt[:, 1, :]
+        filt = filter_ref[c * KX : (c + 1) * KX, :].astype(F32)
+        fr, fi = filt[:, :NZ], filt[:, NZ:]
         grad_r = jnp.zeros((KX, NZ), F32)
         grad_i = jnp.zeros((KX, NZ), F32)
         for y in range(NY):
@@ -408,8 +406,8 @@
             cot_spec.append(jnp.concatenate([gr * fr + gi * fi, gi * fr - gr * fi], axis=1).astype(BF))
             grad_r = grad_r + (gr * sr + gi * si)
             grad_i = grad_i + (gi * sr - gr * si)
-        grad_ref[c * KX : (c + 1) * KX, 0, :] = grad_r
-        grad_ref[c * KX : (c + 1) * KX, 1, :] = grad_i
+        grad_ref[c * KX : (c + 1) * KX, :NZ] = grad_r
+        grad_ref[c * KX : (c + 1) * KX, NZ:] = grad_i
     for field, parts in enumerate((filtered, cot_spec)):
         planes = lax.dot_general(
             table, jnp.concatenate(parts, axis=0), NT, preferred_element_type=F32
@@ -424,7 +422,7 @@
         spectral_kernel,
         out_shape=(
             jax.ShapeDtypeStruct((N_SLAB, 2 * ZL, 2 * LINES), BF),
-            jax.ShapeDtypeStruct((CL * KX, 2, NZ), F32),
+            jax.ShapeDtypeStruct((CL * KX, 2 * NZ), F32),
         ),
         in_specs=[VMEM] * 3,
         out_specs=(VMEM,) * 2,
@@ -536,7 +534,7 @@
 
     got = over("row", pack(atom_feats, cotangent, block_tiles, cell_offsets, live_counts))
     cols, rows, infos, cells, halves = spread(got, table_x)
-    planes, grad = spectral(over("slab", cols), table_z, filter_modes.reshape(CL * KX, 2, NZ))
+    planes, grad = spectral(over("slab", cols), table_z, filter_modes.reshape(CL * KX, 2 * NZ))
     found = gather(rows, infos, over("slab", planes), table_x, cells, halves)
     long_range, grad_feats = unpack(over("row", found))
     return (long_range, grad_feats, grad.reshape(CL, KX, 2, NZ))

time: 140 us -> 142 us (1.014)
  blocking collectives: 123 us -> 66.6 us
  waiting for transfers between devices: 0 us -> 43.3 us
  starting transfers between devices: 0 us -> 13.7 us
    all_to_all x4 -> x2, blocking collectives: 123 us -> 66.6 us  [over(): return lax.all_to_all(values, axis, split_axis=0, concat_axis=0, tiled=True)]
    all_to_all x0 -> x2, waiting for transfers between devices: none -> 43.3 us  [over(): return lax.all_to_all(values, axis, split_axis=0, concat_axis=0, tiled=True)]
    all_to_all x0 -> x2, starting transfers between devices: none -> 13.7 us  [over(): return lax.all_to_all(values, axis, split_axis=0, concat_axis=0, tiled=True)]
  transfers between devices with their start and end apart: 0 -> 2, of which waited for: 0 -> 2; matrix products, arithmetic and copies ran while one was open for 0% -> 1% of each run, Pallas kernels for 0% -> 0%
where the time goes in v6:
time: 142 us
  blocking collectives  66.6 us (47%)
  waiting for transfers between devices  43.3 us (30%)
  Pallas kernels  16.1 us (11%)
  starting transfers between devices  13.7 us (10%)
    all_to_all x2, blocking collectives, over(): return lax.all_to_all(values, axis, split_axis=0, concat_axis=0, tiled=True)  66.6 us
    all_to_all x2, waiting for transfers between devices, over(): return lax.all_to_all(values, axis, split_axis=0, concat_axis=0, tiled=True)  43.3 us
    all_to_all x2, starting transfers between devices, over(): return lax.all_to_all(values, axis, split_axis=0, concat_axis=0, tiled=True)  13.7 us
    pallas_call x1, Pallas kernels, spread(): pl.pallas_call(spread_kernel, out_shape=(jax.ShapeDtypeStruct((N_SLAB, 2...  7.29 us
    pallas_call x1, Pallas kernels, gather(): pl.pallas_call(gather_kernel, out_shape=jax.ShapeDtypeStruct((N_ROW, LT,...  4.98 us
  transfers between devices with their start and end apart: 2, of which 2 were waited for; matrix products, arithmetic and copies ran while one was open for 1% of the time, Pallas kernels for 0%

profile of v6, /device:TPU:1, one launch (start us, length us, event | category | flops | bytes accessed | tf_op | source)
XLA Modules:
  0.0 141.8 jit_solution(8517994976976160166)
XLA Ops:
  1.3 1.9 %pack.1 = bf16[32,9,8,128]{3,2,1,0:T(8,128)(2,1)} custom-call(s32[32]{0:T(128)} %bitcast.10, s32[1,1]{1,0:T(1,128)} %bitcast.6.live_hbm, bf16[128,1024]{1,0:T(8,128)(2,1)} %feat_hbm.1, bf16[128,1024]{1,0:T(8,128)(2,1)} %cot_hbm.1, s32[8,128]{1,0:T(8,128)} %bitcast.9), custom_call_target="tpu_custom_call" | custom-call | tf_op jit(solution)/shard_map/pack/pallas_call | solution.py:164
  3.2 0.0 copy-start
  3.2 53.2 %all_to_all.20.got_ref = bf16[32,9,8,128]{3,2,1,0:T(8,128)(2,1)S(1)} all-to-all(bf16[32,9,8,128]{3,2,1,0:T(8,128)(2,1)} %pack.1), channel_id=1, replica_groups=mesh['slab'=16,'row'=32] {'row'}, dimensions={0} | all-to-all | bytes 1179648 | tf_op jit(solution)/shard_map/all_to_all | solution.py:533
  56.4 0.0 copy-done
  56.4 7.3 %spread.1 = (bf16[16,32,512]{2,1,0:T(8,128)(2,1)}, s32[296]{0:T(512)S(1)}, s32[8,128]{1,0:T(8,128)S(1)}, f32[264,128]{1,0:T(8,128)S(1)}, f32[264,128]{1,0:T(8,128)S(1)}) custom-call(bf16[32,9,8,128]{3,2,1,0:T(8,128)(2,1)S(1)} %all_to_all.20.got_ref, bf16[256,512]{1,0:T(8,128)(2,1)S(1)} %copy-done), custom_call_target="tpu_custom_call" | custom-call | tf_op jit(solution)/shard_map/spread/pallas_call | solution.py:367
  63.7 0.0 copy-start.2
  63.7 0.0 copy-start.1
  63.7 7.8 %all-to-all-start.1 = ((bf16[16,32,512]{2,1,0:T(8,128)(2,1)}), bf16[16,32,512]{2,1,0:T(8,128)(2,1)S(1)}, u32[]{:S(2)}, u32[]{:S(2)}) async-start(bf16[16,32,512]{2,1,0:T(8,128)(2,1)} %get-tuple-element.14), calls=%async_computation.1 | async-start | bytes 1048576 | tf_op jit(solution)/shard_map/all_to_all | solution.py:533
  71.5 0.0 copy-done.2
  71.6 10.6 %all-to-all-done.1.cols_ref = bf16[16,32,512]{2,1,0:T(8,128)(2,1)S(1)} async-done(((bf16[16,32,512]{2,1,0:T(8,128)(2,1)}), bf16[16,32,512]{2,1,0:T(8,128)(2,1)S(1)}, u32[]{:S(2)}, u32[]{:S(2)}) %all-to-all-start.1) | async-done | bytes 524320 | tf_op jit(solution)/shard_map/all_to_all | solution.py:533
  82.1 0.0 copy-done.1
  82.1 1.0 spectral.1
  83.1 13.4 %all_to_all.21.plane_ref = bf16[16,32,512]{2,1,0:T(8,128)(2,1)S(1)} all-to-all(bf16[16,32,512]{2,1,0:T(8,128)(2,1)S(1)} %get-tuple-element.15), channel_id=1, replica_groups=mesh['slab'=16,'row'=32] {'slab'}, dimensions={0} | all-to-all | bytes 1048576 | tf_op jit(solution)/shard_map/all_to_all | solution.py:533
  96.5 5.0 %gather.1 = bf16[32,8,8,128]{3,2,1,0:T(8,128)(2,1)} custom-call(s32[296]{0:T(512)S(1)} %get-tuple-element.12.list_ref, s32[8,128]{1,0:T(8,128)S(1)} %get-tuple-element.13.info_ref, bf16[16,32,512]{2,1,0:T(8,128)(2,1)S(1)} %all_to_all.21.plane_ref, bf16[256,512]{1,0:T(8,128)(2,1)S(1)} %copy-done, f32[264,128]{1,0:T(8,128)S(1)} %get-tuple-element.16.cell_ref, ...), custom_call_target="tpu_custom_call" | custom-call | tf_op jit(solution)/shard_map/gather/pallas_call | solution.py:513
  101.5 5.9 %all-to-all-start.3 = ((bf16[32,8,8,128]{3,2,1,0:T(8,128)(2,1)}), bf16[32,8,8,128]{3,2,1,0:T(8,128)(2,1)S(1)}, u32[]{:S(2)}, u32[]{:S(2)}) async-start(bf16[32,8,8,128]{3,2,1,0:T(8,128)(2,1)} %gather.1), calls=%async_computation.3 | async-start | bytes 1048576 | tf_op jit(solution)/shard_map/all_to_all | solution.py:533
  107.4 0.7 reshape.25
  108.1 32.8 %all-to-all-done.3.in_ref = bf16[32,8,8,128]{3,2,1,0:T(8,128)(2,1)S(1)} async-done(((bf16[32,8,8,128]{3,2,1,0:T(8,128)(2,1)}), bf16[32,8,8,128]{3,2,1,0:T(8,128)(2,1)S(1)}, u32[]{:S(2)}, u32[]{:S(2)}) %all-to-all-start.3) | async-done | bytes 524320 | tf_op jit(solution)/shard_map/all_to_all | solution.py:533
  140.9 0.9 unpack.1
  (1 shorter events, 0.0 us)
Async XLA Ops:
  3.2 53.2 %copy-start = (bf16[256,512]{1,0:T(8,128)(2,1)S(1)}, bf16[256,512]{1,0:T(8,128)(2,1)}, u32[]{:S(2)}) copy-start(bf16[256,512]{1,0:T(8,128)(2,1)} %constant.9.table_ref) | copy-start | bytes 786436
  63.7 7.9 %copy-start.2 = (bf16[4,16,2,256]{3,2,1,0:T(2,128)(2,1)S(1)}, bf16[4,16,2,256]{3,2,1,0:T(2,128)(2,1)}, u32[]{:S(2)}) copy-start(bf16[4,16,2,256]{3,2,1,0:T(2,128)(2,1)} %param.10) | copy-start | bytes 196612
  63.7 18.4 %copy-start.1 = (bf16[512,512]{1,0:T(8,128)(2,1)S(1)}, bf16[512,512]{1,0:T(8,128)(2,1)}, u32[]{:S(2)}) copy-start(bf16[512,512]{1,0:T(8,128)(2,1)} %constant.10.table_ref) | copy-start | bytes 1572868
  63.7 18.4 %all-to-all-start.1 = ((bf16[16,32,512]{2,1,0:T(8,128)(2,1)}), bf16[16,32,512]{2,1,0:T(8,128)(2,1)S(1)}, u32[]{:S(2)}, u32[]{:S(2)}) async-start(bf16[16,32,512]{2,1,0:T(8,128)(2,1)} %get-tuple-element.14), calls=%async_computation.1 | async-start | bytes 1048576 | tf_op jit(solution)/shard_map/all_to_all | solution.py:533
  101.5 39.4 %all-to-all-start.3 = ((bf16[32,8,8,128]{3,2,1,0:T(8,128)(2,1)}), bf16[32,8,8,128]{3,2,1,0:T(8,128)(2,1)S(1)}, u32[]{:S(2)}, u32[]{:S(2)}) async-start(bf16[32,8,8,128]{3,2,1,0:T(8,128)(2,1)} %gather.1), calls=%async_computation.3 | async-start | bytes 1048576 | tf_op jit(solution)/shard_map/all_to_all | solution.py:533
